TPU v7x, 32 devices: a whole 2x2x4 slice. The times are simulated.
32 devices in a mesh: dp: 8 (over z, x), mp: 4 (over y, core).
Axes of the slice: x: 2, y: 2, z: 4, core: 2. Of those that a mesh axis runs over, the one named last changes fastest.
Arguments:
- tokens: bfloat16 [32, 512, 768], P('dp'), may hold values from -6 to 6
- visible: int32 [32], P('dp'), may hold values from 129 to 512, as said below
- w_query: bfloat16 [768, 768], P(None, 'mp'), may hold values from -0.21875 to 0.21875
- b_query: bfloat16 [768], P('mp'), may hold values from -3 to 3
- w_key: bfloat16 [768, 768], P(None, 'mp'), may hold values from -0.21875 to 0.21875
- w_value: bfloat16 [768, 768], P(None, 'mp'), may hold values from -0.21875 to 0.21875
- b_value: bfloat16 [768], P('mp'), may hold values from -3 to 3
- w_output: bfloat16 [768, 768], P('mp'), may hold values from -1.75 to 1.75
- b_output: bfloat16 [768], replicated, may hold values from -2 to 2
- w_expand: bfloat16 [768, 3072], P(None, 'mp'), may hold values from -0.21875 to 0.21875
- b_expand: bfloat16 [3072], P('mp'), may hold values from -3 to 3
- w_reduce: bfloat16 [3072, 768], P('mp'), may hold values from -0.21875 to 0.21875
- b_reduce: bfloat16 [768], replicated, may hold values from -2 to 2
- gain_first: bfloat16 [768], replicated, may hold values from 0.5 to 1.5
- shift_first: bfloat16 [768], replicated, may hold values from -2 to 2
- gain_second: bfloat16 [768], replicated, may hold values from 0.5 to 1.5
- shift_second: bfloat16 [768], replicated, may hold values from -2 to 2
- cotangent: bfloat16 [32, 512, 768], P('dp'), may hold values from -6 to 6
Outputs:
- result: bfloat16 [32, 512, 768], P('dp')
- grad_tokens: bfloat16 [32, 512, 768], P('dp')
- grad_query: float32 [768, 768], P('dp', 'mp')
- grad_bquery: float32 [768], P('mp')
- grad_key: float32 [768, 768], P('dp', 'mp')
- grad_value: float32 [768, 768], P('dp', 'mp')
- grad_bvalue: float32 [768], P('mp')
- grad_output: float32 [768, 768], P('mp', 'dp')
- grad_boutput: float32 [768], replicated
- grad_expand: float32 [768, 3072], P('dp', 'mp')
- grad_bexpand: float32 [3072], P('mp')
- grad_reduce: float32 [3072, 768], P('mp', 'dp')
- grad_breduce: float32 [768], replicated
- grad_gain_first: float32 [768], replicated
- grad_shift_first: float32 [768], replicated
- grad_gain_second: float32 [768], replicated
- grad_shift_second: float32 [768], replicated
Inputs may be any that keep to these rules, and one draw needn't show every extreme that they name: Number of visible patches of each strip, the other of its 512 slots being padding; in every aligned block of 4 strips one strip has all 512 slots visible.
All inputs are finite; a program needn't handle non-finite values.
Results may differ from a plain program's by a relative error of at most 0.018.
Values may be sent and summed in bfloat16 or wider, within the bound.
No kernel may reach another device: no remote copies, remote signals or barrier semaphores. Data moves between devices by JAX's collectives and lax.ppermute only.
A program may use at most 192 MiB of HBM per device.

v0:
```python
from functools import partial

import jax
import jax.numpy as jnp
from jax import lax
from jax.sharding import PartitionSpec as P

HD = 64


def layer_norm(values, gain, shift):
    center = values - jnp.mean(values, axis=-1, keepdims=True)
    spread = jnp.mean(center * center, axis=-1, keepdims=True)
    return center * lax.rsqrt(spread + 1e-06) * gain + shift


def matmul(left, right):
    return jnp.dot(left, right, preferred_element_type=jnp.float32)


def left_product(left, right):
    return jnp.einsum("rd,re->de", left, right, preferred_element_type=jnp.float32)


def right_product(left, right):
    return jnp.einsum("re,de->rd", left, right, preferred_element_type=jnp.float32)


def local(
    tokens,
    visible,
    w_query,
    b_query,
    w_key,
    w_value,
    b_value,
    w_output,
    b_output,
    w_expand,
    b_expand,
    w_reduce,
    b_reduce,
    gain_first,
    shift_first,
    gain_second,
    shift_second,
    cotangent,
):
    strips_here, slots, width = tokens.shape
    heads_here = w_query.shape[1] // HD
    rows_here = strips_here * slots
    scale = HD ** (-0.5)
    valid = jnp.arange(slots, dtype=jnp.int32)[None, :] < visible[:, None]
    row_mask = valid.reshape(rows_here, 1).astype(jnp.float32)
    source = tokens.astype(jnp.float32).reshape(rows_here, width)
    gain_one_f = gain_first.astype(jnp.float32)
    shift_one_f = shift_first.astype(jnp.float32)
    gain_two_f = gain_second.astype(jnp.float32)
    shift_two_f = shift_second.astype(jnp.float32)
    normed_one, pull_first = jax.vjp(layer_norm, source, gain_one_f, shift_one_f)
    normed_low = normed_one.astype(jnp.bfloat16)
    queries = (matmul(normed_low, w_query) + b_query.astype(jnp.float32)).astype(jnp.bfloat16)
    keys_low = matmul(normed_low, w_key).astype(jnp.bfloat16)
    values_low = (matmul(normed_low, w_value) + b_value.astype(jnp.float32)).astype(jnp.bfloat16)
    queries = queries.reshape(strips_here, slots, heads_here, HD)
    keys_low = keys_low.reshape(strips_here, slots, heads_here, HD)
    values_low = values_low.reshape(strips_here, slots, heads_here, HD)

    def masked_scores():
        raw = (
            jnp.einsum("sqhd,skhd->shqk", queries, keys_low, preferred_element_type=jnp.float32)
            * scale
        )
        return jnp.where(valid[:, None, None, :], raw, -1e30)

    scores = masked_scores()
    top_score = jnp.max(scores, axis=-1, keepdims=True)
    log_total = top_score + jnp.log(jnp.sum(jnp.exp(scores - top_score), axis=-1, keepdims=True))
    probs_low = jnp.exp(scores - log_total).astype(jnp.bfloat16)
    context = jnp.einsum(
        "shqk,skhd->sqhd", probs_low, values_low, preferred_element_type=jnp.float32
    )
    context = context.astype(jnp.bfloat16).reshape(rows_here, heads_here * HD)
    attn_sum = lax.psum(matmul(context, w_output).astype(jnp.bfloat16), "mp").astype(jnp.float32)
    resid = source + attn_sum + b_output.astype(jnp.float32)
    normed_two, pull_second = jax.vjp(layer_norm, resid, gain_two_f, shift_two_f)
    normed_two_low = normed_two.astype(jnp.bfloat16)
    pre_act = matmul(normed_two_low, w_expand) + b_expand.astype(jnp.float32)
    activated, pull_gelu = jax.vjp(partial(jax.nn.gelu, approximate=False), pre_act)
    hidden_low = activated.astype(jnp.bfloat16)
    mlp_sum = lax.psum(matmul(hidden_low, w_reduce).astype(jnp.bfloat16), "mp").astype(jnp.float32)
    output = row_mask * (resid + mlp_sum + b_reduce.astype(jnp.float32))
    result = output.astype(jnp.bfloat16).reshape(strips_here, slots, width)
    grad_out = cotangent.astype(jnp.float32).reshape(rows_here, width) * row_mask
    grad_branch = grad_out.astype(jnp.bfloat16)
    d_b_reduce = jnp.sum(grad_branch.astype(jnp.float32), axis=0)
    d_w_reduce = left_product(hidden_low, grad_branch)
    d_hidden = right_product(grad_branch, w_reduce)
    d_pre = pull_gelu(d_hidden)[0].astype(jnp.bfloat16)
    d_b_expand = jnp.sum(d_pre.astype(jnp.float32), axis=0)
    d_w_expand = left_product(normed_two_low, d_pre)
    d_norm_two = lax.psum(right_product(d_pre, w_expand).astype(jnp.bfloat16), "mp").astype(
        jnp.float32
    )
    d_resid_norm, d_gain_two, d_shift_two = pull_second(d_norm_two)
    grad_resid = grad_out + d_resid_norm
    grad_attn = grad_resid.astype(jnp.bfloat16)
    d_b_output = jnp.sum(grad_attn.astype(jnp.float32), axis=0)
    d_w_output = left_product(context, grad_attn)
    d_context = right_product(grad_attn, w_output).astype(jnp.bfloat16)
    d_context = d_context.reshape(strips_here, slots, heads_here, HD)
    probs_again = jnp.exp(masked_scores() - log_total)
    d_probs = jnp.einsum(
        "sqhd,skhd->shqk", d_context, values_low, preferred_element_type=jnp.float32
    )
    d_values = jnp.einsum(
        "shqk,sqhd->skhd",
        probs_again.astype(jnp.bfloat16),
        d_context,
        preferred_element_type=jnp.float32,
    ).astype(jnp.bfloat16)
    row_terms = jnp.sum(probs_again * d_probs, axis=-1, keepdims=True)
    d_scores = (probs_again * (d_probs - row_terms)).astype(jnp.bfloat16)
    d_queries = (
        scale
        * jnp.einsum("shqk,skhd->sqhd", d_scores, keys_low, preferred_element_type=jnp.float32)
    ).astype(jnp.bfloat16)
    d_keys = (
        scale * jnp.einsum("shqk,sqhd->skhd", d_scores, queries, preferred_element_type=jnp.float32)
    ).astype(jnp.bfloat16)
    d_queries = d_queries.reshape(rows_here, heads_here * HD)
    d_keys = d_keys.reshape(rows_here, heads_here * HD)
    d_values = d_values.reshape(rows_here, heads_here * HD)
    d_b_query = jnp.sum(d_queries.astype(jnp.float32), axis=0)
    d_b_value = jnp.sum(d_values.astype(jnp.float32), axis=0)
    d_w_query = left_product(normed_low, d_queries)
    d_w_key = left_product(normed_low, d_keys)
    d_w_value = left_product(normed_low, d_values)
    back_first = (
        right_product(d_queries, w_query)
        + right_product(d_keys, w_key)
        + right_product(d_values, w_value)
    )
    d_norm_one = lax.psum(back_first.astype(jnp.bfloat16), "mp").astype(jnp.float32)
    d_source_norm, d_gain_one, d_shift_one = pull_first(d_norm_one)
    grad_tokens = (
        (grad_resid + d_source_norm).astype(jnp.bfloat16).reshape(strips_here, slots, width)
    )
    all_parts = (
        lax.psum_scatter(d_w_query, "dp", scatter_dimension=0, tiled=True),
        lax.psum_scatter(d_w_key, "dp", scatter_dimension=0, tiled=True),
        lax.psum_scatter(d_w_value, "dp", scatter_dimension=0, tiled=True),
        lax.psum_scatter(d_w_output, "dp", scatter_dimension=1, tiled=True),
        lax.psum_scatter(d_w_expand, "dp", scatter_dimension=0, tiled=True),
        lax.psum_scatter(d_w_reduce, "dp", scatter_dimension=1, tiled=True),
    )
    grad_query, grad_key, grad_value, grad_output, grad_expand, grad_reduce = all_parts
    small_parts = lax.psum(
        (
            d_b_query,
            d_b_value,
            d_b_output,
            d_b_expand,
            d_b_reduce,
            d_gain_one,
            d_shift_one,
            d_gain_two,
            d_shift_two,
        ),
        "dp",
    )
    (
        grad_bquery,
        grad_bvalue,
        grad_boutput,
        grad_bexpand,
        grad_breduce,
        grad_gain_first,
        grad_shift_first,
        grad_gain_second,
        grad_shift_second,
    ) = small_parts
    return (
        result,
        grad_tokens,
        grad_query,
        grad_bquery,
        grad_key,
        grad_value,
        grad_bvalue,
        grad_output,
        grad_boutput,
        grad_expand,
        grad_bexpand,
        grad_reduce,
        grad_breduce,
        grad_gain_first,
        grad_shift_first,
        grad_gain_second,
        grad_shift_second,
    )


def solution(mesh):
    placed = (
        P("dp", None, None),
        P("dp"),
        P(None, "mp"),
        P("mp"),
        P(None, "mp"),
        P(None, "mp"),
        P("mp"),
        P("mp", None),
        P(),
        P(None, "mp"),
        P("mp"),
        P("mp", None),
        P(),
        P(),
        P(),
        P(),
        P(),
        P("dp", None, None),
    )
    return jax.shard_map(
        local,
        mesh=mesh,
        in_specs=placed,
        out_specs=(
            P("dp", None, None),
            P("dp", None, None),
            P("dp", "mp"),
            P("mp"),
            P("dp", "mp"),
            P("dp", "mp"),
            P("mp"),
            P("mp", "dp"),
            P(),
            P("dp", "mp"),
            P("mp"),
            P("mp", "dp"),
            P(),
            P(),
            P(),
            P(),
            P(),
        ),
        check_vma=False,
    )
```

profile of v0, /device:TPU:0, one launch (start us, length us, event | category | flops | bytes accessed | tf_op | source)
XLA Modules:
  0.0 806.8 jit_solution(2346179748115485372)
XLA Ops:
  7.3 0.8 convert_element_type.174
  8.1 0.9 convert_element_type.172
  10.3 2.4 convert_reduce_fusion.2
  12.8 2.9 fusion.18
  17.1 1.3 fusion.17
  18.4 1.7 copy-done.18
  20.1 1.2 fusion.34
  21.8 3.1 convolution_convert_fusion.4
  25.5 4.0 fusion.33
  29.4 2.3 reshape.267
  31.7 3.1 fusion
  34.9 3.6 exponential_reduce_fusion
  38.5 0.9 copy-done.5
  39.4 2.9 fusion.35
  43.2 2.7 convolution_convert_fusion.2
  46.8 1.3 convert_element_type.186
  48.1 1.3 convert_element_type.184
  49.4 0.7 copy.85
  50.1 4.1 fusion.28
  54.2 63.0 %all-reduce.6.cloned.1.call-done = bf16[2048,768]{1,0:T(8,128)(2,1)} async-done(((bf16[2048,768]{1,0:T(8,128)(2,1)}), bf16[2048,768]{1,0:T(8,128)(2,1)}) %all-reduce.6.cloned.1.call-update) | async-done | bytes 3145744 | tf_op jit(solution)/shard_map/psum | solution.py:84
  117.2 4.1 fusion.30
  121.9 1.8 multiply_reduce_fusion.1
  124.4 2.9 fusion.61
  127.9 19.2 %convert_reduce_fusion.4 = (f32[768]{0:T(1024)}, bf16[2048,768]{1,0:T(8,128)(2,1)S(1)}, f32[2048,768]{1,0:T(8,128)}) fusion(f32[2048,768]{1,0:T(8,128)S(1)} %fusion.61, f32[768]{0:T(1024)S(1)} %copy-done.61, bf16[2048,768]{1,0:T(8,128)(2,1)S(1)} %copy-done.16, bf16[768,768]{1,0:T(8,128)(2,1)S(1)} %copy-done), kind=kOutput, calls=%fused_computation.44 | convolution fusion | flops 2533883136 | bytes 20060160 | tf_op jit(solution)/shard_map/re,de->rd/dot_general | solution.py:26
  147.1 1.6 copy-done.71
  148.7 4.0 convolution_convert_fusion
  153.2 5.5 multiply_convert_fusion.3
  158.7 1.7 copy-done.19
  160.4 4.0 convolution_convert_fusion.1
  164.4 57.1 %all-reduce.8.cloned.1.call-done = bf16[2048,768]{1,0:T(8,128)(2,1)} async-done(((bf16[2048,768]{1,0:T(8,128)(2,1)}), bf16[2048,768]{1,0:T(8,128)(2,1)}) %all-reduce.8.cloned.1.call-update) | async-done | bytes 3145744 | tf_op jit(solution)/shard_map/psum | solution.py:102
  221.5 5.9 convert_reduce_fusion.1
  228.0 5.3 fusion.9
  233.3 4.4 convert_reduce_fusion.5
  237.7 1.6 copy-done.15
  239.4 2.3 convolution_bitcast_fusion
  241.6 3.1 convolution_convert_fusion.3
  245.3 7.7 convert_reduce_fusion.6
  253.0 9.7 %multiply_reduce_fusion = (f32[4,3,512]{2,1,0:T(4,128)S(1)}, f32[4,3,512,512]{2,3,1,0:T(8,128)}) fusion(f32[4,3,512,512]{2,3,1,0:T(8,128)} %copy-done.5, f32[4,3,512]{2,1,0:T(4,128)S(1)} %copy-done.28, pred[4,512]{1,0:T(4,128)(4,1)S(1)} %get-tuple-element.51, bf16[4,512,3,64]{1,0,3,2:T(4,128)(2,1)S(1)} %copy-done.14, bf16[4,512,3,64]{1,0,3,2:T(4,128)(2,1)S(1)} %reshape.273), kind=kOutput, calls=%fused_computation.1 | convolution fusion | flops 418375680 | bytes 26789888 | tf_op jit(solution)/shard_map/sqhd,skhd->shqk/dot_general | solution.py:113
  262.7 7.4 multiply_convert_fusion
  270.1 2.0 fusion.38
  272.2 1.2 convert_reduce_fusion.7
  274.3 1.0 fusion.65
  277.0 1.0 fusion.66
  278.0 2.8 add_convert_fusion.1
  281.6 2.7 fusion.21
  284.4 1.7 copy-done.17
  286.0 1.9 fusion.69
  288.1 3.8 fusion.68
  292.2 3.8 fusion.67
  296.1 6.9 fusion.70
  303.1 8.0 fusion.60
  311.2 2.6 convert_reduce_fusion.3
  314.0 22.2 %reduce-scatter.19.cloned.1.call-done = f32[96,192]{1,0:T(8,128)} async-done(((f32[768,192]{1,0:T(8,128)}), f32[96,192]{1,0:T(8,128)}) %reduce-scatter.19.cloned.1.call-update) | async-done | bytes 73744
  336.2 1.6 copy.84
  337.8 120.1 %all-reduce.10.cloned.1.call-done = (bf16[2048,768]{1,0:T(8,128)(2,1)}, bf16[2048,768]{1,0:T(8,128)(2,1)}) async-done(((bf16[2048,768]{1,0:T(8,128)(2,1)}, bf16[2048,768]{1,0:T(8,128)(2,1)}), (bf16[2048,768]{1,0:T(8,128)(2,1)}, bf16[2048,768]{1,0:T(8,128)(2,1)})) %all-reduce.10.cloned.1.call-update) | async-done | bytes 6291472 | tf_op jit(solution)/shard_map/psum | solution.py:91
  458.0 4.2 convert_reduce_fusion
  462.3 5.1 fusion.10
  467.5 38.0 %all-reduce = (f32[192]{0:T(256)}, f32[192]{0:T(256)}, f32[768]{0:T(1024)}, f32[768]{0:T(1024)}, f32[768]{0:T(1024)}, /*index=5*/f32[768]{0:T(1024)}, f32[768]{0:T(1024)}, f32[768]{0:T(1024)}, f32[768]{0:T(1024)}) all-reduce(f32[192]{0:T(256)S(1)} %reduce_sum.218, f32[192]{0:T(256)S(1)} %reduce_sum.220, ...), channel_id=1, replica_groups=mesh['dp'=8,'mp'=4] {'dp'}, use_global_device_ids=true, to_apply=%region_17.18 | all-reduce | flops 5760 | bytes 46080 | tf_op jit(solution)/shard_map/psum | solution.py:158
  505.5 11.9 %add_convert_fusion = (bf16[2048,768]{1,0:T(8,128)(2,1)}, bf16[2048,768]{1,0:T(8,128)(2,1)}) fusion(bf16[4,512,768]{2,1,0:T(8,128)(2,1)} %param.18, bf16[2048,768]{1,0:T(8,128)(2,1)} %get-tuple-element.35, bf16[4,512,768]{2,1,0:T(8,128)(2,1)} %param.35, f32[2048]{0:T(1024)S(1)} %negate_multiply_fusion.1, f32[2048]{0:T(1024)S(1)} %multiply_multiply_fusion.5, ...), kind=kLoop, calls=%fused_computation.46 | loop fusion | flops 47185920 | bytes 25251840 | tf_op jit(solution)/shard_map/convert_element_type | solution.py:147
  517.4 7.4 reduce-scatter.13.cloned.1.call-done
  524.8 65.2 %reduce-scatter.11.cloned.1.call-done = f32[96,192]{1,0:T(8,128)} async-done(((f32[768,192]{1,0:T(8,128)}), f32[96,192]{1,0:T(8,128)}) %reduce-scatter.11.cloned.1.call-update) | async-done | bytes 73744 | tf_op jit(solution)/shard_map/reduce_scatter | solution.py:151
  590.0 65.7 %reduce-scatter.9.cloned.1.call-done = f32[96,192]{1,0:T(8,128)} async-done(((f32[768,192]{1,0:T(8,128)}), f32[96,192]{1,0:T(8,128)}) %reduce-scatter.9.cloned.1.call-update) | async-done | bytes 73744 | tf_op jit(solution)/shard_map/reduce_scatter | solution.py:150
  655.7 72.1 %reduce-scatter.17.cloned.1.call-done = f32[768,96]{0,1:T(8,128)} async-done(((f32[768,768]{0,1:T(8,128)}), f32[768,96]{0,1:T(8,128)}) %reduce-scatter.17.cloned.1.call-update) | async-done | bytes 294928 | tf_op jit(solution)/shard_map/reduce_scatter | solution.py:155
  727.8 72.1 %reduce-scatter.15.cloned.1.call-done = f32[96,768]{1,0:T(8,128)} async-done(((f32[768,768]{1,0:T(8,128)}), f32[96,768]{1,0:T(8,128)}) %reduce-scatter.15.cloned.1.call-update) | async-done | bytes 294928 | tf_op jit(solution)/shard_map/reduce_scatter | solution.py:154
  (194 shorter events, 12.9 us)
Async XLA Ops:
  7.2 120.1 %copy-start = (bf16[768,768]{1,0:T(8,128)(2,1)S(1)}, bf16[768,768]{1,0:T(8,128)(2,1)}, u32[]{:S(2)}) copy-start(bf16[768,768]{1,0:T(8,128)(2,1)} %param.29) | copy-start | bytes 3538948
  7.2 9.1 %copy-start.69 = (s32[4]{0:T(128)S(1)}, s32[4]{0:T(128)}, u32[]{:S(2)}) copy-start(s32[4]{0:T(128)} %param.19) | copy-start | bytes 52
  7.2 110.0 %all-reduce.6.cloned.1.call-start = ((), (), s32[]{:S(2)}) async-start(), calls=%async_computation.6 | async-start | bytes 6291456 | tf_op jit(solution)/shard_map/psum | solution.py:84
  7.3 9.8 %copy-start.2 = (bf16[4,512,768]{2,1,0:T(8,128)(2,1)S(1)}, bf16[4,512,768]{2,1,0:T(8,128)(2,1)}, u32[]{:S(2)}) copy-start(bf16[4,512,768]{2,1,0:T(8,128)(2,1)} %param.18) | copy-start | bytes 9437188
  9.6 8.7 %copy-start.31 = (f32[768]{0:T(1024)}, f32[768]{0:T(1024)S(1)}, u32[]{:S(2)}) copy-start(f32[768]{0:T(1024)S(1)} %convert_element_type.169) | copy-start | bytes 9220
  10.3 8.0 copy-start.54
  10.3 9.8 %copy-start.21 = (bf16[768,192]{0,1:T(8,128)(2,1)S(1)}, bf16[768,192]{0,1:T(8,128)(2,1)}, u32[]{:S(2)}) copy-start(bf16[768,192]{0,1:T(8,128)(2,1)} %param.20) | copy-start | bytes 884740
  12.7 5.6 copy-start.48
  12.8 5.6 copy-start.29
  31.7 6.8 copy-start.13
  34.9 4.5 copy-start.5
  39.4 3.8 copy-start.24
  43.0 3.2 copy-start.65
  43.0 3.2 copy-start.66
  45.9 175.5 %all-reduce.8.cloned.1.call-start = ((), (), s32[]{:S(2)}) async-start(), calls=%async_computation.7 | async-start | bytes 6291456 | tf_op jit(solution)/shard_map/psum | solution.py:102
  50.1 67.2 %copy-start.33 = (f32[1,4,4,128]{3,1,2,0:T(4,128)}, f32[1,4,4,128]{3,1,2,0:T(4,128)S(1)}, u32[]{:S(2)}) copy-start(f32[1,4,4,128]{3,1,2,0:T(4,128)S(1)} %copy.85) | copy-start | bytes 24580
  117.2 4.1 copy-start.3
  117.2 4.7 copy-start.6
  123.7 3.5 copy-start.11
  124.3 3.0 copy-start.36
  124.3 3.5 copy-start.16
  124.3 3.5 copy-start.61
  127.9 19.2 %copy-start.12 = (f32[2048,768]{1,0:T(8,128)}, f32[2048,768]{1,0:T(8,128)S(1)}, u32[]{:S(2)}) copy-start(f32[2048,768]{1,0:T(8,128)S(1)} %fusion.61) | copy-start | bytes 18874372
  152.8 183.4 %reduce-scatter.19.cloned.1.call-start = ((), (), s32[]{:S(2)}) async-start(), calls=%async_computation.13 | async-start | bytes 884736
  164.4 63.1 %copy-start.53 = (f32[2048]{0:T(1024)S(1)}, f32[2048]{0:T(1024)}, u32[]{:S(2)}) copy-start(f32[2048]{0:T(1024)} %copy-done.52) | copy-start | bytes 24580
  164.4 63.1 %copy-start.37 = (f32[2048]{0:T(1024)S(1)}, f32[2048]{0:T(1024)}, u32[]{:S(2)}) copy-start(f32[2048]{0:T(1024)} %copy-done.36) | copy-start | bytes 24580
  164.4 63.1 %copy-start.44 = (f32[768]{0:T(1024)S(1)}, f32[768]{0:T(1024)}, u32[]{:S(2)}) copy-start(f32[768]{0:T(1024)} %convert_element_type.183) | copy-start | bytes 9220
  221.5 6.0 copy-start.4
  221.5 6.0 copy-start.7
  221.5 6.5 copy-start.8
  227.4 5.9 copy-start.9
  227.4 5.9 copy-start.34
  228.0 9.7 %copy-start.39 = (f32[2048]{0:T(1024)}, f32[2048]{0:T(1024)S(1)}, u32[]{:S(2)}) copy-start(f32[2048]{0:T(1024)S(1)} %multiply_multiply_fusion.6) | copy-start | bytes 24580
  233.3 4.4 copy-start.46
  233.3 8.3 %copy-start.25 = (bf16[192,768]{1,0:T(8,128)(2,1)S(1)}, bf16[192,768]{1,0:T(8,128)(2,1)}, u32[]{:S(2)}) copy-start(bf16[192,768]{1,0:T(8,128)(2,1)} %param.25) | copy-start | bytes 884740
  239.4 5.9 copy-start.28
  245.3 7.7 copy-start.14
  245.3 17.5 %slice-start = ((s8[12582912]{0:T(1024)(128)(4,1)}), s8[4194304]{0:T(1024)(128)(4,1)S(1)}, s32[]{:S(2)}) async-start(s8[12582912]{0:T(1024)(128)(4,1)} %bitcast.142), calls=%async_computation.15 | async-start | bytes 8388608
  245.3 17.4 %slice-start.1 = ((s8[12582912]{0:T(1024)(128)(4,1)}), s8[4194304]{0:T(1024)(128)(4,1)S(1)}, s32[]{:S(2)}) async-start(s8[12582912]{0:T(1024)(128)(4,1)} %bitcast.142), calls=%async_computation.16 | async-start | bytes 8388608
  253.0 9.8 %slice-start.2 = ((s8[12582912]{0:T(1024)(128)(4,1)}), s8[4194304]{0:T(1024)(128)(4,1)S(1)}, s32[]{:S(2)}) async-start(s8[12582912]{0:T(1024)(128)(4,1)} %bitcast.142), calls=%async_computation.17 | async-start | bytes 8388608
  273.4 184.5 %all-reduce.10.cloned.1.call-start = ((), (), s32[]{:S(2)}) async-start(), calls=%async_computation.14 | async-start | bytes 12582912 | tf_op jit(solution)/shard_map/psum | solution.py:91
  280.9 243.8 %reduce-scatter.13.cloned.1.call-start = ((), (), s32[]{:S(2)}) async-start(), calls=%async_computation.10 | async-start | bytes 884736 | tf_op jit(solution)/shard_map/reduce_scatter | solution.py:152
  288.0 302.0 %reduce-scatter.11.cloned.1.call-start = ((), (), s32[]{:S(2)}) async-start(), calls=%async_computation.9 | async-start | bytes 884736 | tf_op jit(solution)/shard_map/reduce_scatter | solution.py:151
  291.9 363.8 %reduce-scatter.9.cloned.1.call-start = ((), (), s32[]{:S(2)}) async-start(), calls=%async_computation.8 | async-start | bytes 884736 | tf_op jit(solution)/shard_map/reduce_scatter | solution.py:150
  296.0 7.1 copy-start.64
  296.0 431.8 %reduce-scatter.17.cloned.1.call-start = ((), (), s32[]{:S(2)}) async-start(), calls=%async_computation.12 | async-start | bytes 2654208 | tf_op jit(solution)/shard_map/reduce_scatter | solution.py:155
  303.0 8.1 %copy-start.67 = (bf16[768]{0:T(1024)(128)(2,1)S(1)}, bf16[768]{0:T(1024)(128)(2,1)}, u32[]{:S(2)}) copy-start(bf16[768]{0:T(1024)(128)(2,1)} %param.30) | copy-start | bytes 4612
  303.0 8.1 %copy-start.57 = (f32[4,512]{1,0:T(4,128)S(1)}, f32[4,512]{1,0:T(4,128)}, u32[]{:S(2)}) copy-start(f32[4,512]{1,0:T(4,128)} %get-tuple-element.49) | copy-start | bytes 24580
  303.1 10.7 %copy-start.68 = (f32[3,64]{1,0:T(4,128)S(1)}, f32[3,64]{1,0:T(4,128)}, u32[]{:S(2)}) copy-start(f32[3,64]{1,0:T(4,128)} %get-tuple-element.58) | copy-start | bytes 2308
  303.1 154.9 %copy-start.30 = (f32[1,4,4,128]{3,1,2,0:T(4,128)S(1)}, f32[1,4,4,128]{3,1,2,0:T(4,128)}, u32[]{:S(2)}) copy-start(f32[1,4,4,128]{3,1,2,0:T(4,128)} %copy-done.29) | copy-start | bytes 24580
  303.1 496.8 %reduce-scatter.15.cloned.1.call-start = ((), (), s32[]{:S(2)}) async-start(), calls=%async_computation.11 | async-start | bytes 2654208 | tf_op jit(solution)/shard_map/reduce_scatter | solution.py:154
  311.1 151.1 %copy-start.51 = (f32[1,4,4,128]{3,1,2,0:T(4,128)S(1)}, f32[1,4,4,128]{3,1,2,0:T(4,128)}, u32[]{:S(2)}) copy-start(f32[1,4,4,128]{3,1,2,0:T(4,128)} %copy-done.50) | copy-start | bytes 24580
  311.1 151.2 %copy-start.42 = (f32[2048]{0:T(1024)S(1)}, f32[2048]{0:T(1024)}, u32[]{:S(2)}) copy-start(f32[2048]{0:T(1024)} %copy-done.41) | copy-start | bytes 24580
  457.9 4.4 copy-start.10
  457.9 9.5 %copy-start.58 = (f32[768]{0:T(1024)S(1)}, f32[768]{0:T(1024)}, u32[]{:S(2)}) copy-start(f32[768]{0:T(1024)} %get-tuple-element.21) | copy-start | bytes 9220
  457.9 9.5 %copy-start.59 = (f32[768]{0:T(1024)S(1)}, f32[768]{0:T(1024)}, u32[]{:S(2)}) copy-start(f32[768]{0:T(1024)} %get-tuple-element.17) | copy-start | bytes 9220
  458.0 9.5 %copy-start.60 = (f32[768]{0:T(1024)S(1)}, f32[768]{0:T(1024)}, u32[]{:S(2)}) copy-start(f32[768]{0:T(1024)} %get-tuple-element.39) | copy-start | bytes 9220
  458.0 9.5 %copy-start.62 = (f32[768]{0:T(1024)S(1)}, f32[768]{0:T(1024)}, u32[]{:S(2)}) copy-start(f32[768]{0:T(1024)} %get-tuple-element.36) | copy-start | bytes 9220
  458.0 47.5 %copy-start.35 = (f32[1,4,4,128]{3,1,2,0:T(4,128)S(1)}, f32[1,4,4,128]{3,1,2,0:T(4,128)}, u32[]{:S(2)}) copy-start(f32[1,4,4,128]{3,1,2,0:T(4,128)} %copy-done.33) | copy-start | bytes 24580
  458.0 47.5 %copy-start.38 = (f32[2048]{0:T(1024)S(1)}, f32[2048]{0:T(1024)}, u32[]{:S(2)}) copy-start(f32[2048]{0:T(1024)} %copy-done.36) | copy-start | bytes 24580
  458.0 47.4 %copy-start.40 = (f32[2048]{0:T(1024)S(1)}, f32[2048]{0:T(1024)}, u32[]{:S(2)}) copy-start(f32[2048]{0:T(1024)} %copy-done.39) | copy-start | bytes 24580
  458.0 47.4 %copy-start.45 = (f32[768]{0:T(1024)S(1)}, f32[768]{0:T(1024)}, u32[]{:S(2)}) copy-start(f32[768]{0:T(1024)} %convert_element_type.183) | copy-start | bytes 9220
  458.0 47.4 %copy-start.47 = (f32[2048]{0:T(1024)S(1)}, f32[2048]{0:T(1024)}, u32[]{:S(2)}) copy-start(f32[2048]{0:T(1024)} %copy-done.46) | copy-start | bytes 24580
  505.5 294.4 %copy-start.1 = (bf16[768,768]{1,0:T(8,128)(2,1)S(1)}, bf16[768,768]{1,0:T(8,128)(2,1)}, u32[]{:S(2)}) copy-start(bf16[768,768]{1,0:T(8,128)(2,1)} %param.29) | copy-start | bytes 3538948
  (20 other events, 33.3 us)
Sparse Core Ops, SparseCore 0:
  46.1 71.1 all-reduce.5
  152.9 68.5 all-reduce.7
  273.6 62.5 reduce-scatter.18
  339.1 118.7 all-reduce.9
  462.0 62.7 reduce-scatter.12
  528.5 61.4 reduce-scatter.10
  594.2 61.4 reduce-scatter.8
  659.8 67.9 reduce-scatter.16
  731.9 67.9 reduce-scatter.14
where the time goes:
time: 816 us; the launch traced here: 807 us
  waiting for transfers between devices  545 us (67%)
  matrix products  103 us (13%)
  other arithmetic  82.8 us (10%)
  blocking collectives  38 us (5%)
  local copies, waits for them, and re-layouts  22 us (3%)
  between operations  15.2 us (2%)
    psum x1, waiting for transfers between devices, local(): lax.psum(matmul(hidden_low, w_reduce).astype(jnp.bfloat16), 'mp')  120 us
    reduce_scatter x1, waiting for transfers between devices, local(): lax.psum_scatter(d_w_reduce, 'dp', scatter_dimension=1, tiled=True)  72.1 us
    reduce_scatter x1, waiting for transfers between devices, local(): lax.psum_scatter(d_w_expand, 'dp', scatter_dimension=0, tiled=True)  72.1 us
    reduce_scatter x1, waiting for transfers between devices, local(): lax.psum_scatter(d_w_query, 'dp', scatter_dimension=0, tiled=True)  65.7 us
    reduce_scatter x1, waiting for transfers between devices, local(): lax.psum_scatter(d_w_key, 'dp', scatter_dimension=0, tiled=True)  65.2 us
    psum x1, waiting for transfers between devices, local(): lax.psum(matmul(context, w_output).astype(jnp.bfloat16), 'mp')  63 us
    psum x1, waiting for transfers between devices, local(): lax.psum(right_product(d_pre, w_expand).astype(jnp.bfloat16), 'mp')  57.1 us
    psum x1, blocking collectives, local(): lax.psum((d_b_query, d_b_value, d_b_output, d_b_expand, d_b_reduce, d_gai...  38 us
  transfers between devices with their start and end apart: 9, of which 9 were waited for; matrix products, arithmetic and copies ran while one was open for 10% of the time, Pallas kernels for 0%

commit v1 on v0

v1 whole, which is shorter than its diff:
```python
from functools import partial

import jax
import jax.numpy as jnp
from jax import lax
from jax.experimental import pallas as pl
from jax.experimental.pallas import tpu as pltpu
from jax.sharding import PartitionSpec as P

HD = 64
F32 = jnp.float32
BF = jnp.bfloat16
NT = (((1,), (1,)), ((), ()))
VMEM = pl.BlockSpec(memory_space=pltpu.VMEM)
SMEM = pl.BlockSpec(memory_space=pltpu.SMEM)


def dot(left, right):
    return jnp.dot(left, right, preferred_element_type=F32)


def dot_nt(left, right):
    return lax.dot_general(left, right, NT, preferred_element_type=F32)


def shape(dims, dtype):
    return jax.ShapeDtypeStruct(dims, dtype)


def call(body, outs, args, flops, limit=48, scratch=()):
    specs = [SMEM if a.dtype == jnp.int32 else VMEM for a in args]
    moved = sum(a.size * a.dtype.itemsize for a in list(args) + list(outs))
    return pl.pallas_call(
        body,
        in_specs=specs,
        out_shape=tuple(outs),
        scratch_shapes=list(scratch),
        cost_estimate=pl.CostEstimate(flops=flops, bytes_accessed=moved, transcendentals=0),
        compiler_params=pltpu.CompilerParams(vmem_limit_bytes=limit << 20),
    )(*args)


def norm_parts(values):
    center = values - jnp.mean(values, axis=-1, keepdims=True)
    rstd = lax.rsqrt(jnp.mean(center * center, axis=-1, keepdims=True) + 1e-06)
    return center * rstd, rstd


def norm_back(unit, rstd, gain, grad):
    scaled = grad * gain
    first = jnp.mean(scaled, axis=-1, keepdims=True)
    second = jnp.mean(scaled * unit, axis=-1, keepdims=True)
    return rstd * (scaled - first - unit * second)


def row_sum(values):
    return jnp.sum(values, axis=0, keepdims=True)


def norm_one_body(tok, gain, shift, normed, normed_t):
    unit, _ = norm_parts(tok[...].astype(F32))
    low = (unit * gain[...].astype(F32) + shift[...].astype(F32)).astype(BF)
    normed[...] = low
    normed_t[...] = low.T


def norm_one(tok, gain, shift):
    rows, width = tok.shape
    outs = (shape((rows, width), BF), shape((width, rows), BF))
    return call(norm_one_body, outs, (tok, gain, shift), 10 * rows * width)


def attn_fwd_body(slots, visible, normed, *refs):
    wq, wk, wv = refs[:slots], refs[slots : 2 * slots], refs[2 * slots : 3 * slots]
    small = refs[3 * slots : 4 * slots]
    q_out, k_out, v_out, e_out, o_out, ctx_out = refs[4 * slots :]
    rows, _ = normed.shape
    part = wq[0].shape[1]
    heads = part // HD
    lane = lax.broadcasted_iota(jnp.int32, (rows, HD), 1)
    row = lax.broadcasted_iota(jnp.int32, (rows, HD), 0)
    one = jnp.where(lane == 0, 1.0, 0.0).astype(BF)
    mask = jnp.where((lane == 0) & (row >= visible[0]), -1e30, 0.0).astype(BF)
    low = normed[...]
    for s in range(slots):
        q = ((dot(low, wq[s][...]) + small[s][1:2, :part].astype(F32)).astype(BF) * BF(HD**-0.5))
        k = dot(low, wk[s][...]).astype(BF)
        v = (dot(low, wv[s][...]) + small[s][1:2, part : 2 * part].astype(F32)).astype(BF)
        for h in range(heads):
            cols = slice(h * HD, (h + 1) * HD)
            i = s * heads + h
            q_out[i, :, :HD] = q[:, cols]
            q_out[i, :, HD:] = one
            k_out[i, :, :HD] = k[:, cols]
            k_out[i, :, HD:] = mask
            v_out[i, :, :HD] = v[:, cols]
            v_out[i, :, HD:] = one
    for i in range(slots * heads):
        scores = dot_nt(q_out[i], k_out[i])
        e = jnp.exp(scores - jnp.max(scores, axis=1, keepdims=True)).astype(BF)
        e_out[i] = e
        o = dot(e, v_out[i])
        o_out[i] = o
        ctx_out[:, i * HD : (i + 1) * HD] = (o[:, :HD] * (1.0 / o[:, HD : HD + 1])).astype(BF)


def attn_fwd(visible, normed, wq, wk, wv, small):
    slots = len(wq)
    rows, width = normed.shape
    part = wq[0].shape[1]
    n = slots * part // HD
    outs = [shape((n, rows, 2 * HD), BF)] * 3
    outs += [shape((n, rows, rows), BF), shape((n, rows, 2 * HD), F32), shape((rows, n * HD), BF)]
    flops = 2 * rows * width * 3 * slots * part + 2 * n * 2 * rows * rows * HD
    return call(partial(attn_fwd_body, slots), outs, (visible, normed, *wq, *wk, *wv, *small), flops)


def middle_body(pairs, visible, tok, cot, bias, gain, shift, *refs):
    ctx, wo = refs[:pairs], refs[pairs : pairs + 2 * pairs]
    resid, normed, normed_t, branch, branch_t, d_bias = refs[3 * pairs :]
    rows, _ = tok.shape
    part = wo[0].shape[0]
    total = tok[...].astype(F32) + bias[...].astype(F32)
    for p in range(pairs):
        for s in range(2):
            total += dot(ctx[p][:, s * part : (s + 1) * part], wo[2 * p + s][...])
    resid[...] = total
    unit, _ = norm_parts(total)
    low = (unit * gain[...].astype(F32) + shift[...].astype(F32)).astype(BF)
    normed[...] = low
    normed_t[...] = low.T
    row = lax.broadcasted_iota(jnp.int32, cot.shape, 0)
    kept = jnp.where(row < visible[0], cot[...].astype(F32), 0.0)
    branch[...] = kept.astype(BF)
    branch_t[...] = kept.astype(BF).T
    d_bias[...] = row_sum(kept)


def middle(visible, tok, cot, bias, gain, shift, ctx, wo):
    rows, width = tok.shape
    flat, tall = shape((rows, width), BF), shape((width, rows), BF)
    outs = (shape((rows, width), F32), flat, tall, flat, tall, shape((1, width), F32))
    args = (visible, tok, cot, bias, gain, shift, *ctx, *wo)
    return call(partial(middle_body, len(ctx)), outs, args, 2 * rows * width * width)


def ffn_body(slots, carried, normed, normed_t, branch, branch_t, *refs):
    we, wr, small = refs[:slots], refs[slots : 2 * slots], refs[2 * slots : 3 * slots]
    refs = refs[3 * slots :]
    carry, refs = refs[: 2 * carried], refs[2 * carried :]
    grads, d_small, mlp, d_norm = refs[:slots], refs[slots], refs[slots + 1], refs[slots + 2]
    units = we[0].shape[1]
    for s in range(slots):
        pre = dot(normed[...], we[s][...]) + small[s][0:1, :].astype(F32)
        cdf = 0.5 * (1.0 + lax.erf(pre * 0.7071067811865476))
        slope = cdf + pre * (jnp.exp(-0.5 * pre * pre) * 0.3989422804014327)
        hidden = (pre * cdf).astype(BF)
        d_pre = (dot_nt(branch[...], wr[s][...]) * slope).astype(BF)
        d_small[s : s + 1, :] = row_sum(d_pre.astype(F32))
        out = dot(hidden, wr[s][...])
        back = dot_nt(d_pre, we[s][...])
        if s == 0 and not carried:
            mlp[...] = out
            d_norm[...] = back
        elif s == 0:
            mlp[...] = carry[0][...] + out
            d_norm[...] = carry[1][...] + back
        else:
            mlp[...] += out
            d_norm[...] += back
        grads[s][:, :units] = dot(normed_t[...], d_pre).astype(BF)
        grads[s][:, units:] = dot(branch_t[...], hidden).astype(BF)


def ffn(normed, normed_t, branch, branch_t, we, wr, small, carry=()):
    slots = len(we)
    rows, width = normed.shape
    units = we[0].shape[1]
    outs = [shape((width, 2 * units), BF)] * slots + [shape((8, units), F32)] + [shape((rows, width), F32)] * 2
    args = (normed, normed_t, branch, branch_t, *we, *wr, *small, *carry)
    return call(partial(ffn_body, slots, len(carry) // 2), outs, args, 12 * rows * width * units * slots)


def turn_body(visible, resid, mlp, bias, d_norm, branch, gain, result, grad, attn, attn_t, sums):
    row = lax.broadcasted_iota(jnp.int32, resid.shape, 0)
    base = resid[...]
    total = base + (mlp[...] + bias[...].astype(F32))
    result[...] = jnp.where(row < visible[0], total, 0.0).astype(BF)
    unit, rstd = norm_parts(base)
    dn = d_norm[...]
    g = branch[...].astype(F32) + norm_back(unit, rstd, gain[...].astype(F32), dn)
    grad[...] = g
    low = g.astype(BF)
    attn[...] = low
    attn_t[...] = low.T
    sums[0:1, :] = row_sum(low.astype(F32))
    sums[1:2, :] = row_sum(dn * unit)
    sums[2:3, :] = row_sum(dn)


def turn(visible, resid, mlp, bias, d_norm, branch, gain):
    rows, width = resid.shape
    outs = (shape((rows, width), BF), shape((rows, width), F32), shape((rows, width), BF))
    outs += (shape((width, rows), BF), shape((8, width), F32))
    return call(turn_body, outs, (visible, resid, mlp, bias, d_norm, branch, gain), 30 * rows * width)


def attn_bwd_body(slots, carried, attn, attn_t, normed_t, q_in, k_in, v_in, e_in, o_in, ctx, *refs):
    wo, wq, wk, wv = (refs[i * slots : (i + 1) * slots] for i in range(4))
    refs = refs[4 * slots :]
    carry, refs = refs[:carried], refs[carried:]
    grads, d_small, d_norm = refs[:slots], refs[slots], refs[slots + 1]
    d_in = refs[slots + 2]
    rows, _ = attn.shape
    part = wq[0].shape[1]
    heads = part // HD
    lane = lax.broadcasted_iota(jnp.int32, (rows, HD), 1)
    for s in range(slots):
        d_ctx = dot_nt(attn[...], wo[s][...]).astype(BF).astype(F32)
        back_v, back_k = [], []
        for h in range(heads):
            i = s * heads + h
            o = o_in[i]
            inverse = 1.0 / o[:, HD : HD + 1]
            do = (d_ctx[:, h * HD : (h + 1) * HD] * inverse).astype(BF)
            term = jnp.sum(do.astype(F32) * o[:, :HD], axis=1, keepdims=True) * inverse
            e = e_in[i]
            d_prob = dot_nt(do, v_in[i][:, :HD])
            d_score = (e.astype(F32) * (d_prob - term)).astype(BF)
            back_v.append(dot(do.T, e))
            back_k.append(dot(q_in[i][:, :HD].T, d_score))
            d_in[:, h * HD : (h + 1) * HD] = (dot(d_score, k_in[i][:, :HD]) * HD**-0.5).astype(BF)
        d_in[:, part : 2 * part] = jnp.concatenate(back_k, axis=0).T.astype(BF)
        d_in[:, 2 * part : 3 * part] = jnp.concatenate(back_v, axis=0).T.astype(BF)
        dq, dk, dv = (d_in[:, i * part : (i + 1) * part] for i in range(3))
        d_small[s : s + 1, :part] = row_sum(dq.astype(F32))
        d_small[s : s + 1, part : 2 * part] = row_sum(dv.astype(F32))
        back = dot_nt(dq, wq[s][...]) + dot_nt(dk, wk[s][...]) + dot_nt(dv, wv[s][...])
        if s == 0 and not carried:
            d_norm[...] = back
        elif s == 0:
            d_norm[...] = carry[0][...] + back
        else:
            d_norm[...] += back
        grads[s][:, : 3 * part] = dot(normed_t[...], d_in[...]).astype(BF)
        grads[s][:, 3 * part :] = dot(attn_t[...], ctx[:, s * part : (s + 1) * part]).astype(BF)


def attn_bwd(attn, attn_t, normed_t, saved, wo, wq, wk, wv, carry=()):
    slots = len(wq)
    rows, width = attn.shape
    part = wq[0].shape[1]
    outs = [shape((width, 4 * part), BF)] * slots + [shape((8, width), F32), shape((rows, width), F32)]
    args = (attn, attn_t, normed_t, *saved, *wo, *wq, *wk, *wv, *carry)
    flops = slots * part * (16 * rows * width + 10 * rows * rows)
    scratch = (pltpu.VMEM((rows, 3 * part), BF),)
    return call(partial(attn_bwd_body, slots, len(carry)), outs, args, flops, 50, scratch)


def norm_one_back_body(tok, gain, d_norm, grad, out, sums):
    unit, rstd = norm_parts(tok[...].astype(F32))
    dn = d_norm[...]
    out[...] = (grad[...] + norm_back(unit, rstd, gain[...].astype(F32), dn)).astype(BF)
    sums[0:1, :] = row_sum(dn * unit)
    sums[1:2, :] = row_sum(dn)


def norm_one_back(tok, gain, d_norm, grad):
    rows, width = tok.shape
    outs = (shape((rows, width), BF), shape((8, width), F32))
    return call(norm_one_back_body, outs, (tok, gain, d_norm, grad), 20 * rows * width)


def swap(values, axis, size, bit):
    return lax.ppermute(values, axis, [(i, i ^ (1 << bit)) for i in range(size)])


def pick(values, index, axis):
    return lax.dynamic_index_in_dim(values, index, axis, keepdims=False)


def scatter_sum(values, size, index):
    width = values.shape[-1]
    block = values.shape[-2] // size
    lead = values.shape[:-2]
    for bit in range(size.bit_length() - 1):
        size_now = size >> bit
        split = values.reshape(*lead, size_now // 2, 2, block, width)
        mine = (index >> bit) & 1
        away = pick(split, 1 - mine, len(lead) + 1)
        kept = pick(split, mine, len(lead) + 1)
        got = swap(away, "dp", size, bit)
        values = (kept.astype(F32) + got.astype(F32)).astype(values.dtype)
    return values.reshape(*lead, block, width)


def spread_body(index, *refs):
    ins, out, sem = refs[:4], refs[4], refs[5]
    copies = [pltpu.make_async_copy(ins[s], out.at[index[0] ^ s], sem.at[s]) for s in range(4)]
    for copy in copies:
        copy.start()
    for copy in copies:
        copy.wait()


def spread(index, strips):
    rows, width = strips[0].shape
    return pl.pallas_call(
        spread_body,
        in_specs=[SMEM] + [pl.BlockSpec(memory_space=pl.ANY)] * 4,
        out_specs=pl.BlockSpec(memory_space=pl.ANY),
        out_shape=shape((4, rows, width), strips[0].dtype),
        scratch_shapes=[pltpu.SemaphoreType.DMA((4,))],
    )(index, *strips)


def local(
    sizes,
    tokens,
    visible,
    w_query,
    b_query,
    w_key,
    w_value,
    b_value,
    w_output,
    b_output,
    w_expand,
    b_expand,
    w_reduce,
    b_reduce,
    gain_first,
    shift_first,
    gain_second,
    shift_second,
    cotangent,
):
    n_dp, n_mp = sizes
    dp, mp = lax.axis_index("dp"), lax.axis_index("mp")
    part, units, width = w_query.shape[1], w_expand.shape[1], tokens.shape[2]
    core = partial(swap, axis="mp", size=n_mp, bit=0)
    across = partial(swap, axis="mp", size=n_mp, bit=1)

    def gather(own):
        near, far = core(own), across(own)
        return [own, near, far, core(far)]

    def flat(vector):
        return vector.reshape(1, -1)

    tok, cot = pick(tokens, mp, 0), pick(cotangent, mp, 0)
    vis = pick(visible, mp, 0).reshape(1)
    small_own = jnp.zeros((16, units), BF)
    small_own = small_own.at[0].set(b_expand)
    small_own = small_own.at[1, :part].set(b_query).at[1, part : 2 * part].set(b_value)
    small = gather(small_own)
    wq, wk, wv = gather(w_query), gather(w_key), gather(w_value)
    wo = gather(w_output)
    we, wr = gather(w_expand), gather(w_reduce)

    n1, n1t = norm_one(tok, flat(gain_first), flat(shift_first))
    near = attn_fwd(vis, n1, wq[:2], wk[:2], wv[:2], small[:2])
    away = attn_fwd(vis, n1, wq[2:], wk[2:], wv[2:], small[2:])
    resid, n2, n2t, branch, branch_t, d_reduce = middle(
        vis, tok, cot, flat(b_output), flat(gain_second), flat(shift_second), (near[5], away[5]), wo
    )
    g0, g1, de_near, mlp, dn2 = ffn(n2, n2t, branch, branch_t, we[:2], wr[:2], small[:2])
    got0 = core(g1)
    g2, g3, de_away, mlp, dn2 = ffn(
        n2, n2t, branch, branch_t, we[2:], wr[2:], small[2:], (mlp, dn2)
    )
    got2 = core(g3)
    strip, grad_resid, attn, attn_t, sums2 = turn(
        vis, resid, mlp, flat(b_reduce), dn2, branch, flat(gain_second)
    )
    result = spread(mp.reshape(1), gather(strip))

    def add(left, right):
        return (left.astype(F32) + right.astype(F32)).astype(BF)

    def finish(left, right):
        return left.astype(F32) + right.astype(F32)

    expand_sum = add(add(g0[:, :units], got0[:, :units]), across(add(g2[:, :units], got2[:, :units])))
    grad_expand = scatter_sum(expand_sum, n_dp, dp).astype(F32)
    reduce_sum = jnp.stack([add(g0[:, units:], got0[:, units:]), add(g2[:, units:], got2[:, units:])])
    reduce_sum = scatter_sum(reduce_sum, n_dp, dp)
    grad_reduce = finish(reduce_sum[0], across(reduce_sum[1])).T

    h2, h3, ds_away, dn1 = attn_bwd(attn, attn_t, n1t, away, wo[2:], wq[2:], wk[2:], wv[2:])
    sum2 = scatter_sum(add(h2, core(h3)), n_dp, dp)
    h0, h1, ds_near, dn1 = attn_bwd(attn, attn_t, n1t, near, wo[:2], wq[:2], wk[:2], wv[:2], (dn1,))
    sum0 = scatter_sum(add(h0, core(h1)), n_dp, dp)
    heads_sum = finish(sum0, across(sum2))
    grad_query, grad_key = heads_sum[:, :part], heads_sum[:, part : 2 * part]
    grad_value, grad_output = heads_sum[:, 2 * part : 3 * part], heads_sum[:, 3 * part :].T
    grad_strip, sums1 = norm_one_back(tok, flat(gain_first), dn1, grad_resid)
    grad_tokens = spread(mp.reshape(1), gather(grad_strip))

    slots = [jnp.stack([e, s]) for e, s in zip([*de_near[:2], *de_away[:2]], [*ds_near[:2], *ds_away[:2]])]
    shared = jnp.concatenate([d_reduce, sums2[:3], sums1[:2]])
    got = core(jnp.concatenate([slots[1], slots[3], shared]))
    slots0, slots2, shared = slots[0] + got[:2], slots[2] + got[2:4], shared + got[4:]
    got = across(jnp.concatenate([slots2, shared]))
    totals = jnp.concatenate([slots0, shared]) + got
    for bit in range(n_dp.bit_length() - 1):
        totals = totals + swap(totals, "dp", n_dp, bit)
    return (
        result,
        grad_tokens,
        grad_query,
        totals[1, :part],
        grad_key,
        grad_value,
        totals[1, part : 2 * part],
        grad_output,
        totals[3],
        grad_expand,
        totals[0],
        grad_reduce,
        totals[2],
        totals[6],
        totals[7],
        totals[4],
        totals[5],
    )


def solution(mesh):
    placed = (
        P("dp", None, None),
        P("dp"),
        P(None, "mp"),
        P("mp"),
        P(None, "mp"),
        P(None, "mp"),
        P("mp"),
        P("mp", None),
        P(),
        P(None, "mp"),
        P("mp"),
        P("mp", None),
        P(),
        P(),
        P(),
        P(),
        P(),
        P("dp", None, None),
    )
    return jax.shard_map(
        partial(local, (mesh.shape["dp"], mesh.shape["mp"])),
        mesh=mesh,
        in_specs=placed,
        out_specs=(
            P("dp", None, None),
            P("dp", None, None),
            P("dp", "mp"),
            P("mp"),
            P("dp", "mp"),
            P("dp", "mp"),
            P("mp"),
            P("mp", "dp"),
            P(),
            P("dp", "mp"),
            P("mp"),
            P("mp", "dp"),
            P(),
            P(),
            P(),
            P(),
            P(),
        ),
        check_vma=False,
    )
```

time: 816 us -> 533 us (0.65)
  waiting for transfers between devices: 545 us -> 161 us
  Pallas kernels: 0 us -> 275 us
  matrix products: 103 us -> 0 us
  other arithmetic: 82.8 us -> 20.3 us
  starting transfers between devices: 1.2 us -> 39.5 us
  blocking collectives: 38 us -> 0 us
  between operations: 15.2 us -> 1.71 us
    reduce_scatter x5 -> x0, waiting for transfers between devices: 283 us -> none  [the longest x1 72.1 us: local(): lax.psum_scatter(d_w_reduce, 'dp', scatter_dimension=1, tiled=True)]
    pallas_call x0 -> x12, Pallas kernels: none -> 275 us  [the longest x2 193 us: spread(): pl.pallas_call(spread_body, in_specs=[SMEM] + [pl.BlockSpec(memory_space=...]
    psum x3 -> x0, waiting for transfers between devices: 240 us -> none  [the longest x1 120 us: local(): lax.psum(matmul(hidden_low, w_reduce).astype(jnp.bfloat16), 'mp')]
    ppermute x0 -> x51, waiting for transfers between devices: none -> 161 us  [swap(): return lax.ppermute(values, axis, [(i, i ^ 1 << bit) for i in range(size)])]
    dot_general x23 -> x0, matrix products: 100 us -> none  [the longest x6 31.2 us: right_product(): jnp.einsum('re,de->rd', left, right, preferred_element_type=jnp.float32)]
    reduce_sum x11 -> x0, other arithmetic: 42.4 us -> none  [the longest x4 20.6 us: layer_norm(): return center * lax.rsqrt(spread + 1e-06) * gain + shift]
    ppermute x0 -> x51, starting transfers between devices: none -> 39.5 us  [swap(): return lax.ppermute(values, axis, [(i, i ^ 1 << bit) for i in range(size)])]
    psum x1 -> x0, blocking collectives: 38 us -> none  [local(): lax.psum((d_b_query, d_b_value, d_b_output, d_b_expand, d_b_reduce, d_gai...]
  transfers between devices with their start and end apart: 9 -> 51, of which waited for: 9 -> 20; matrix products, arithmetic and copies ran while one was open for 10% -> 6% of each run, Pallas kernels for 0% -> 50%
where the time goes in v1:
time: 533 us; the launch traced here: 523 us
  Pallas kernels  275 us (52%)
  waiting for transfers between devices  161 us (30%)
  starting transfers between devices  39.5 us (7%)
  local copies, waits for them, and re-layouts  25.6 us (5%)
  other arithmetic  20.3 us (4%)
    pallas_call x2, Pallas kernels, spread(): pl.pallas_call(spread_body, in_specs=[SMEM] + [pl.BlockSpec(memory_space=...  193 us
    ppermute x51, waiting for transfers between devices, swap(): return lax.ppermute(values, axis, [(i, i ^ 1 << bit) for i in range(size)])  161 us
    pallas_call x10, Pallas kernels, call(): pl.pallas_call(body, in_specs=specs, out_shape=tuple(outs), scratch_shape...  82 us
    ppermute x51, starting transfers between devices, swap(): return lax.ppermute(values, axis, [(i, i ^ 1 << bit) for i in range(size)])  39.5 us
    unnamed x92, local copies, waits for them, and re-layouts  15.6 us
  transfers between devices with their start and end apart: 51, of which 20 were waited for; matrix products, arithmetic and copies ran while one was open for 6% of the time, Pallas kernels for 50%

profile of v1, /device:TPU:0, one launch (start us, length us, event | category | flops | bytes accessed | tf_op | source)
XLA Modules:
  0.0 522.8 jit_solution(6998096431754283180)
XLA Ops:
  0.7 1.2 copy.53.refs_0_.refs_2_
  1.9 3.0 collective-permute-start.4
  7.7 6.8 %collective-permute-done.10.refs_6_.refs_4_ = bf16[16,768]{1,0:T(8,128)(2,1)S(1)} collective-permute-done((bf16[16,768]{1,0:T(8,128)(2,1)S(1)}, bf16[16,768]{1,0:T(8,128)(2,1)S(1)}, u32[]{:S(2)}, u32[]{:S(2)}) %collective-permute-start.10) | collective-permute-done | bytes 24608 | tf_op jit(solution)/shard_map/ppermute | solution.py:275
  14.5 1.1 copy.54.refs_2_.refs_4_
  15.7 1.8 collective-permute-start.6
  18.6 9.1 %collective-permute-done.6.refs_2_.refs_4_ = bf16[768,192]{1,0:T(8,128)(2,1)S(1)} collective-permute-done((bf16[768,192]{1,0:T(8,128)(2,1)S(1)}, bf16[768,192]{1,0:T(8,128)(2,1)S(1)}, u32[]{:S(2)}, u32[]{:S(2)}) %collective-permute-start.6) | collective-permute-done | bytes 294944 | tf_op jit(solution)/shard_map/ppermute | solution.py:275
  27.7 1.7 collective-permute-start.15
  29.4 6.8 %collective-permute-done.8.refs_4_.refs_6_ = bf16[768,192]{1,0:T(8,128)(2,1)} collective-permute-done((bf16[768,192]{1,0:T(8,128)(2,1)S(1)}, bf16[768,192]{1,0:T(8,128)(2,1)}, u32[]{:S(2)}, u32[]{:S(2)}) %collective-permute-start.8) | collective-permute-done | bytes 294944 | tf_op jit(solution)/shard_map/ppermute | solution.py:275
  36.2 1.7 collective-permute-start.17
  38.8 53.8 %collective-permute-done.13.refs_4_.refs_0_ = bf16[192,768]{1,0:T(8,128)(2,1)S(1)} collective-permute-done((bf16[192,768]{1,0:T(8,128)(2,1)S(1)}, bf16[192,768]{1,0:T(8,128)(2,1)S(1)}, u32[]{:S(2)}, u32[]{:S(2)}) %collective-permute-start.13) | collective-permute-done | bytes 294944 | tf_op jit(solution)/shard_map/ppermute | solution.py:275
  93.9 2.9 collective-permute-done.7.refs_3_.refs_5_
  97.7 1.9 collective-permute-done.9.refs_5_.refs_7_
  99.8 2.4 dynamic-slice_bitcast_fusion
  104.9 6.4 %shard_map.306 = (bf16[6,512,128]{2,1,0:T(8,128)(2,1)S(1)}, bf16[6,512,128]{2,1,0:T(8,128)(2,1)S(1)}, bf16[6,512,128]{2,1,0:T(8,128)(2,1)S(1)}, bf16[6,512,512]{...) custom-call(s32[1]{0:T(128)} %dynamic_slice.73.visible, ...), custom_call_target="tpu_custom_call" | custom-call | flops 1308622848 | bytes 10076164 | tf_op jit(solution)/shard_map/pallas_call | solution.py:33
  111.4 0.9 copy-done.7
  114.1 7.6 %shard_map.307 = (bf16[6,512,128]{2,1,0:T(8,128)(2,1)S(1)}, bf16[6,512,128]{2,1,0:T(8,128)(2,1)S(1)}, bf16[6,512,128]{2,1,0:T(8,128)(2,1)S(1)}, bf16[6,512,512]{...) custom-call(s32[1]{0:T(128)} %dynamic_slice.73.visible, ...), custom_call_target="tpu_custom_call" | custom-call | flops 1308622848 | bytes 10076164 | tf_op jit(solution)/shard_map/pallas_call | solution.py:33
  121.7 0.9 copy-done.10
  123.5 0.9 copy-done.12
  124.4 4.2 shard_map.308
  128.6 12.3 %shard_map.309 = (bf16[768,1536]{1,0:T(8,128)(2,1)}, bf16[768,1536]{1,0:T(8,128)(2,1)}, f32[8,768]{1,0:T(8,128)S(1)}, f32[512,768]{1,0:T(8,128)}, f32[512,768]{1,0:T(8,128)}) custom-call(bf16[512,768]{1,0:T(8,128)(2,1)S(1)} %get-tuple-element.102.normed, bf16[768,512]{1,0:T(8,128)(2,1)S(1)} %get-tuple-element.103.normed_t, ...), custom_call_target="tpu_custom_call" | custom-call | flops 7247757312 | bytes 15802368 | tf_op jit(solution)/shard_map/pallas_call | solution.py:33
  141.0 13.6 %shard_map.310 = (bf16[768,1536]{1,0:T(8,128)(2,1)}, bf16[768,1536]{1,0:T(8,128)(2,1)}, f32[8,768]{1,0:T(8,128)S(1)}, f32[512,768]{1,0:T(8,128)}, f32[512,768]{1,0:T(8,128)}) custom-call(bf16[512,768]{1,0:T(8,128)(2,1)S(1)} %get-tuple-element.102.normed, bf16[768,512]{1,0:T(8,128)(2,1)S(1)} %get-tuple-element.103.normed_t, ...), custom_call_target="tpu_custom_call" | custom-call | flops 7247757312 | bytes 18948096 | tf_op jit(solution)/shard_map/pallas_call | solution.py:33
  155.0 4.5 shard_map.311
  159.5 1.0 copy-done.1
  160.5 1.0 copy-done.2
  161.5 15.5 %shard_map.313 = (bf16[768,768]{1,0:T(8,128)(2,1)}, bf16[768,768]{1,0:T(8,128)(2,1)}, f32[8,768]{1,0:T(8,128)S(1)}, f32[512,768]{1,0:T(8,128)}) custom-call(bf16[512,768]{1,0:T(8,128)(2,1)} %copy-done.1, bf16[768,512]{1,0:T(8,128)(2,1)} %copy-done.2, bf16[768,512]{1,0:T(8,128)(2,1)} %copy-done, bf16[6,512,128]{2,1,0:T(8,128)(2,1)} %copy-done.10, ...), custom_call_target="tpu_custom_call" | custom-call | flops 3422552064 | bytes 16146432 | tf_op jit(solution)/shard_map/pallas_call | solution.py:33
  177.2 16.0 %shard_map.314 = (bf16[768,768]{1,0:T(8,128)(2,1)}, bf16[768,768]{1,0:T(8,128)(2,1)}, f32[8,768]{1,0:T(8,128)S(1)}, f32[512,768]{1,0:T(8,128)}) custom-call(bf16[512,768]{1,0:T(8,128)(2,1)} %copy-done.1, bf16[768,512]{1,0:T(8,128)(2,1)} %copy-done.2, bf16[768,512]{1,0:T(8,128)(2,1)} %copy-done, bf16[6,512,128]{2,1,0:T(8,128)(2,1)} %copy-done.7, ...), custom_call_target="tpu_custom_call" | custom-call | flops 3422552064 | bytes 17719296 | tf_op jit(solution)/shard_map/pallas_call | solution.py:33
  193.1 1.4 copy-done.3
  194.5 1.1 shard_map.315
  197.2 1.8 collective-permute-start.37
  199.0 2.1 collective-permute-done.37
  201.1 1.8 collective-permute-start.38
  202.9 2.1 collective-permute-done.38
  205.0 1.8 collective-permute-start.39
  206.8 1.6 add_convert_fusion.5
  208.4 1.6 collective-permute-start.32
  210.1 1.7 add_convert_fusion.6
  211.8 1.0 dynamic-slice_bitcast_fusion.5
  212.8 1.5 collective-permute-start.28
  214.3 3.3 add_convert_fusion
  217.6 1.5 collective-permute-start.43
  219.1 2.7 collective-permute-start.40
  221.8 2.3 collective-permute-done.40
  224.9 1.5 fusion.7
  226.4 8.1 %collective-permute-done.28 = bf16[4,96,768]{2,1,0:T(8,128)(2,1)} collective-permute-done((bf16[4,96,768]{2,1,0:T(8,128)(2,1)}, bf16[4,96,768]{2,1,0:T(8,128)(2,1)}, u32[]{:S(2)}, u32[]{:S(2)}) %collective-permute-start.28) | collective-permute-done | bytes 589856 | tf_op jit(solution)/shard_map/ppermute | solution.py:275
  234.9 1.4 fusion.8
  236.3 24.5 %collective-permute-done.25.refs_2_ = bf16[512,768]{1,0:T(8,128)(2,1)} collective-permute-done((bf16[512,768]{1,0:T(8,128)(2,1)S(1)}, bf16[512,768]{1,0:T(8,128)(2,1)}, u32[]{:S(2)}, u32[]{:S(2)}) %collective-permute-start.25) | collective-permute-done | bytes 786464 | tf_op jit(solution)/shard_map/ppermute | solution.py:275
  260.8 1.5 collective-permute-start.22
  263.0 2.6 collective-permute-start.34
  265.6 3.7 add_convert_fusion.1
  269.3 1.3 fusion.2
  270.7 6.3 %collective-permute-done.22.refs_2_ = bf16[512,768]{1,0:T(8,128)(2,1)} collective-permute-done((bf16[512,768]{1,0:T(8,128)(2,1)S(1)}, bf16[512,768]{1,0:T(8,128)(2,1)}, u32[]{:S(2)}, u32[]{:S(2)}) %collective-permute-start.22) | collective-permute-done | bytes 786464 | tf_op jit(solution)/shard_map/ppermute | solution.py:275
  279.3 2.6 collective-permute-start.30
  281.9 1.5 collective-permute-start.35
  284.7 96.4 %shard_map.316 = bf16[4,512,768]{2,1,0:T(8,128)(2,1)} custom-call(s32[1]{0:T(128)} %bitcast.index, bf16[512,768]{1,0:T(8,128)(2,1)} %copy-done.6, bf16[512,768]{1,0:T(8,128)(2,1)} %copy-done.35, bf16[512,768]{1,0:T(8,128)(2,1)} %collective-permute-done.25.refs_2_, bf16[512,768]{1,0:T(8,128)(2,1)} %collective-permute-done.26.refs_3_), custom_call_target="tpu_custom_call" | custom-call | tf_op jit(solution)/shard_map/pallas_call | solution.py:308
  381.2 96.4 %shard_map.312 = bf16[4,512,768]{2,1,0:T(8,128)(2,1)} custom-call(s32[1]{0:T(128)} %bitcast.index, bf16[512,768]{1,0:T(8,128)(2,1)} %copy-done.5, bf16[512,768]{1,0:T(8,128)(2,1)} %collective-permute-done.21.refs_1_, bf16[512,768]{1,0:T(8,128)(2,1)} %collective-permute-done.22.refs_2_, bf16[512,768]{1,0:T(8,128)(2,1)} %collective-permute-done.23.refs_3_), custom_call_target="tpu_custom_call" | custom-call | tf_op jit(solution)/shard_map/pallas_call | solution.py:308
  477.8 1.4 collective-permute-start.44
  479.1 1.6 fusion
  483.6 8.8 %collective-permute-done.44 = bf16[4,96,768]{2,1,0:T(8,128)(2,1)} collective-permute-done((bf16[4,96,768]{2,1,0:T(8,128)(2,1)S(1)}, bf16[4,96,768]{2,1,0:T(8,128)(2,1)}, u32[]{:S(2)}, u32[]{:S(2)}) %collective-permute-start.44) | collective-permute-done | bytes 589856 | tf_op jit(solution)/shard_map/ppermute | solution.py:275
  492.4 1.2 fusion.6
  494.2 3.3 collective-permute-done.48
  497.5 1.2 fusion.5
  499.1 6.4 %collective-permute-done.45 = bf16[2,96,768]{2,1,0:T(8,128)(2,1)S(1)} collective-permute-done((bf16[2,96,768]{2,1,0:T(8,128)(2,1)S(1)}, bf16[2,96,768]{2,1,0:T(8,128)(2,1)S(1)}, u32[]{:S(2)}, u32[]{:S(2)}) %collective-permute-start.45) | collective-permute-done | bytes 294944 | tf_op jit(solution)/shard_map/ppermute | solution.py:275
  505.7 10.7 %collective-permute-done.49 = bf16[2,1,96,768]{3,2,1,0:T(8,128)(2,1)S(1)} collective-permute-done((bf16[2,1,96,768]{3,2,1,0:T(8,128)(2,1)S(1)}, bf16[2,1,96,768]{3,2,1,0:T(8,128)(2,1)S(1)}, u32[]{:S(2)}, u32[]{:S(2)}) %collective-permute-start.49) | collective-permute-done | bytes 294944 | tf_op jit(solution)/shard_map/ppermute | solution.py:275
  518.7 3.0 collective-permute-done.50
  (203 shorter events, 27.5 us)
Async XLA Ops:
  0.7 16.8 %copy-start.36 = (bf16[768,192]{0,1:T(8,128)(2,1)S(1)}, bf16[768,192]{0,1:T(8,128)(2,1)}, u32[]{:S(2)}) copy-start(bf16[768,192]{0,1:T(8,128)(2,1)} %param.29) | copy-start | bytes 884740
  0.7 37.3 %copy-start.4 = (bf16[192,768]{1,0:T(8,128)(2,1)S(1)}, bf16[192,768]{1,0:T(8,128)(2,1)}, u32[]{:S(2)}) copy-start(bf16[192,768]{1,0:T(8,128)(2,1)} %refs_0_.4) | copy-start | bytes 884740
  1.9 16.7 %collective-permute-start.4 = (bf16[768,192]{1,0:T(8,128)(2,1)S(1)}, bf16[768,192]{1,0:T(8,128)(2,1)}, u32[]{:S(2)}, u32[]{:S(2)}) collective-permute-start(bf16[768,192]{1,0:T(8,128)(2,1)S(1)} %copy.53.refs_0_.refs_2_), channel_id=1, source_target_pairs={{0,2},{1,3},{2,0},{3,1},{4,6},{5,7},{6,4},{7,5},{8,10},{9,11},{10,... | collective-permute-start | bytes 884744 | tf_op jit(solution)/shard_map/ppermute | solution.py:275
  7.6 7.0 %collective-permute-start.10 = (bf16[16,768]{1,0:T(8,128)(2,1)S(1)}, bf16[16,768]{1,0:T(8,128)(2,1)S(1)}, u32[]{:S(2)}, u32[]{:S(2)}) collective-permute-start(bf16[16,768]{1,0:T(8,128)(2,1)S(1)} %scatter.14.refs_6_.refs_4_), channel_id=1, source_target_pairs={{0,2},{1,3},{2,0},{3,1},{4,6},{5,7},{6,4},{7,5},{8,10},{9,11},{10,... | collective-permute-start | bytes 73736 | tf_op jit(solution)/shard_map/ppermute | solution.py:275
  7.6 10.4 %collective-permute-start.3 = (bf16[16,768]{1,0:T(8,128)(2,1)S(1)}, bf16[16,768]{1,0:T(8,128)(2,1)S(1)}, u32[]{:S(2)}, u32[]{:S(2)}) collective-permute-start(bf16[16,768]{1,0:T(8,128)(2,1)S(1)} %scatter.14.refs_6_.refs_4_), channel_id=1, source_target_pairs={{0,1},{1,0},{2,3},{3,2},{4,5},{5,4},{6,7},{7,6},{8,9},{9,8},{10,11... | collective-permute-start | bytes 73736 | tf_op jit(solution)/shard_map/ppermute | solution.py:275
  14.5 3.5 collective-permute-start.11
  15.7 12.0 %collective-permute-start.6 = (bf16[768,192]{1,0:T(8,128)(2,1)S(1)}, bf16[768,192]{1,0:T(8,128)(2,1)S(1)}, u32[]{:S(2)}, u32[]{:S(2)}) collective-permute-start(bf16[768,192]{1,0:T(8,128)(2,1)S(1)} %copy.54.refs_2_.refs_4_), channel_id=1, source_target_pairs={{0,2},{1,3},{2,0},{3,1},{4,6},{5,7},{6,4},{7,5},{8,10},{9,11},{10,... | collective-permute-start | bytes 884744 | tf_op jit(solution)/shard_map/ppermute | solution.py:275
  17.7 18.5 %collective-permute-start.8 = (bf16[768,192]{1,0:T(8,128)(2,1)S(1)}, bf16[768,192]{1,0:T(8,128)(2,1)}, u32[]{:S(2)}, u32[]{:S(2)}) collective-permute-start(bf16[768,192]{1,0:T(8,128)(2,1)S(1)} %copy.55.refs_4_.refs_6_), channel_id=1, source_target_pairs={{0,2},{1,3},{2,0},{3,1},{4,6},{5,7},{6,4},{7,5},{8,10},{9,11},{10,... | collective-permute-start | bytes 884744 | tf_op jit(solution)/shard_map/ppermute | solution.py:275
  18.0 19.9 %collective-permute-start = (bf16[768,192]{1,0:T(8,128)(2,1)S(1)}, bf16[768,192]{1,0:T(8,128)(2,1)S(1)}, u32[]{:S(2)}, u32[]{:S(2)}) collective-permute-start(bf16[768,192]{1,0:T(8,128)(2,1)S(1)} %copy.53.refs_0_.refs_2_), channel_id=1, source_target_pairs={{0,1},{1,0},{2,3},{3,2},{4,5},{5,4},{6,7},{7,6},{8,9},{9,8},{10,11... | collective-permute-start | bytes 884744 | tf_op jit(solution)/shard_map/ppermute | solution.py:275
  18.0 20.2 %collective-permute-start.1 = (bf16[768,192]{1,0:T(8,128)(2,1)S(1)}, bf16[768,192]{1,0:T(8,128)(2,1)S(1)}, u32[]{:S(2)}, u32[]{:S(2)}) collective-permute-start(bf16[768,192]{1,0:T(8,128)(2,1)S(1)} %copy.54.refs_2_.refs_4_), channel_id=1, source_target_pairs={{0,1},{1,0},{2,3},{3,2},{4,5},{5,4},{6,7},{7,6},{8,9},{9,8},{10,11... | collective-permute-start | bytes 884744 | tf_op jit(solution)/shard_map/ppermute | solution.py:275
  18.5 19.8 %collective-permute-start.2 = (bf16[768,192]{1,0:T(8,128)(2,1)S(1)}, bf16[768,192]{1,0:T(8,128)(2,1)S(1)}, u32[]{:S(2)}, u32[]{:S(2)}) collective-permute-start(bf16[768,192]{1,0:T(8,128)(2,1)S(1)} %copy.55.refs_4_.refs_6_), channel_id=1, source_target_pairs={{0,1},{1,0},{2,3},{3,2},{4,5},{5,4},{6,7},{7,6},{8,9},{9,8},{10,11... | collective-permute-start | bytes 884744 | tf_op jit(solution)/shard_map/ppermute | solution.py:275
  27.7 76.7 %collective-permute-start.15 = (bf16[768,768]{1,0:T(8,128)(2,1)}, bf16[768,768]{1,0:T(8,128)(2,1)}, u32[]{:S(2)}, u32[]{:S(2)}) collective-permute-start(bf16[768,768]{1,0:T(8,128)(2,1)} %refs_0_.3), channel_id=1, source_target_pairs={{0,2},{1,3},{2,0},{3,1},{4,6},{5,7},{6,4},{7,5},{8,10},{9,11},{10,... | collective-permute-start | bytes 3538952 | tf_op jit(solution)/shard_map/ppermute | solution.py:275
  36.2 68.6 %collective-permute-start.17 = (bf16[768,768]{1,0:T(8,128)(2,1)}, bf16[768,768]{1,0:T(8,128)(2,1)}, u32[]{:S(2)}, u32[]{:S(2)}) collective-permute-start(bf16[768,768]{1,0:T(8,128)(2,1)} %refs_2_.5), channel_id=1, source_target_pairs={{0,2},{1,3},{2,0},{3,1},{4,6},{5,7},{6,4},{7,5},{8,10},{9,11},{10,... | collective-permute-start | bytes 3538952 | tf_op jit(solution)/shard_map/ppermute | solution.py:275
  37.9 54.6 %collective-permute-start.13 = (bf16[192,768]{1,0:T(8,128)(2,1)S(1)}, bf16[192,768]{1,0:T(8,128)(2,1)S(1)}, u32[]{:S(2)}, u32[]{:S(2)}) collective-permute-start(bf16[192,768]{1,0:T(8,128)(2,1)S(1)} %copy-done.4), channel_id=1, source_target_pairs={{0,2},{1,3},{2,0},{3,1},{4,6},{5,7},{6,4},{7,5},{8,10},{9,11},{10,... | collective-permute-start | bytes 884744 | tf_op jit(solution)/shard_map/ppermute | solution.py:275
  38.3 66.6 %copy-start.13 = (bf16[768,192]{1,0:T(8,128)(2,1)}, bf16[768,192]{1,0:T(8,128)(2,1)S(1)}, u32[]{:S(2)}) copy-start(bf16[768,192]{1,0:T(8,128)(2,1)S(1)} %collective-permute-done.1.refs_3_.refs_5_) | copy-start | bytes 884740
  38.3 54.3 %collective-permute-start.12 = (bf16[192,768]{1,0:T(8,128)(2,1)S(1)}, bf16[192,768]{1,0:T(8,128)(2,1)S(1)}, u32[]{:S(2)}, u32[]{:S(2)}) collective-permute-start(bf16[192,768]{1,0:T(8,128)(2,1)S(1)} %copy-done.4), channel_id=1, source_target_pairs={{0,1},{1,0},{2,3},{3,2},{4,5},{5,4},{6,7},{7,6},{8,9},{9,8},{10,11... | collective-permute-start | bytes 884744 | tf_op jit(solution)/shard_map/ppermute | solution.py:275
  38.3 66.6 %copy-start.15 = (bf16[768,192]{1,0:T(8,128)(2,1)}, bf16[768,192]{1,0:T(8,128)(2,1)S(1)}, u32[]{:S(2)}) copy-start(bf16[768,192]{1,0:T(8,128)(2,1)S(1)} %collective-permute-done.2.refs_5_.refs_7_) | copy-start | bytes 884740
  38.3 54.8 %collective-permute-start.5 = (bf16[768,192]{1,0:T(8,128)(2,1)}, bf16[768,192]{1,0:T(8,128)(2,1)S(1)}, u32[]{:S(2)}, u32[]{:S(2)}) collective-permute-start(bf16[768,192]{1,0:T(8,128)(2,1)} %collective-permute-done.4.refs_0_.refs_2_), channel_id=1, source_target_pairs={{0,1},{1,0},{2,3},{3,2},{4,5},{5,4},{6,7},{7,6},{8,9},{9,8},{10,11... | collective-permute-start | bytes 884744 | tf_op jit(solution)/shard_map/ppermute | solution.py:275
  92.6 36.1 %collective-permute-start.19 = (bf16[768,768]{1,0:T(8,128)(2,1)}, bf16[768,768]{1,0:T(8,128)(2,1)}, u32[]{:S(2)}, u32[]{:S(2)}) collective-permute-start(bf16[768,768]{1,0:T(8,128)(2,1)} %refs_0_.3), channel_id=1, source_target_pairs={{0,1},{1,0},{2,3},{3,2},{4,5},{5,4},{6,7},{7,6},{8,9},{9,8},{10,11... | collective-permute-start | bytes 3538952 | tf_op jit(solution)/shard_map/ppermute | solution.py:275
  92.6 36.0 %collective-permute-start.20 = (bf16[768,768]{1,0:T(8,128)(2,1)}, bf16[768,768]{1,0:T(8,128)(2,1)}, u32[]{:S(2)}, u32[]{:S(2)}) collective-permute-start(bf16[768,768]{1,0:T(8,128)(2,1)} %refs_2_.5), channel_id=1, source_target_pairs={{0,1},{1,0},{2,3},{3,2},{4,5},{5,4},{6,7},{7,6},{8,9},{9,8},{10,11... | collective-permute-start | bytes 3538952 | tf_op jit(solution)/shard_map/ppermute | solution.py:275
  93.8 2.9 collective-permute-start.7
  97.6 2.1 collective-permute-start.9
  99.6 24.8 %collective-permute-start.14 = (bf16[192,768]{1,0:T(8,128)(2,1)S(1)}, bf16[192,768]{1,0:T(8,128)(2,1)S(1)}, u32[]{:S(2)}, u32[]{:S(2)}) collective-permute-start(bf16[192,768]{1,0:T(8,128)(2,1)S(1)} %collective-permute-done.13.refs_4_.refs_0_), channel_id=1, source_target_pairs={{0,1},{1,0},{2,3},{3,2},{4,5},{5,4},{6,7},{7,6},{8,9},{9,8},{10,11... | collective-permute-start | bytes 884744 | tf_op jit(solution)/shard_map/ppermute | solution.py:275
  104.4 36.5 %collective-permute-start.16 = (bf16[768,768]{1,0:T(8,128)(2,1)}, bf16[768,768]{1,0:T(8,128)(2,1)S(1)}, u32[]{:S(2)}, u32[]{:S(2)}) collective-permute-start(bf16[768,768]{1,0:T(8,128)(2,1)} %collective-permute-done.15.refs_0_), channel_id=1, source_target_pairs={{0,1},{1,0},{2,3},{3,2},{4,5},{5,4},{6,7},{7,6},{8,9},{9,8},{10,11... | collective-permute-start | bytes 3538952 | tf_op jit(solution)/shard_map/ppermute | solution.py:275
  104.8 36.2 %collective-permute-start.18 = (bf16[768,768]{1,0:T(8,128)(2,1)}, bf16[768,768]{1,0:T(8,128)(2,1)}, u32[]{:S(2)}, u32[]{:S(2)}) collective-permute-start(bf16[768,768]{1,0:T(8,128)(2,1)} %collective-permute-done.17.refs_2_), channel_id=1, source_target_pairs={{0,1},{1,0},{2,3},{3,2},{4,5},{5,4},{6,7},{7,6},{8,9},{9,8},{10,11... | collective-permute-start | bytes 3538952 | tf_op jit(solution)/shard_map/ppermute | solution.py:275
  154.6 59.7 %collective-permute-start.42 = (bf16[768,1536]{1,0:T(8,128)(2,1)}, bf16[768,1536]{1,0:T(8,128)(2,1)}, u32[]{:S(2)}, u32[]{:S(2)}) collective-permute-start(bf16[768,1536]{1,0:T(8,128)(2,1)} %get-tuple-element.142), channel_id=1, source_target_pairs={{0,1},{1,0},{2,3},{3,2},{4,5},{5,4},{6,7},{7,6},{8,9},{9,8},{10,11... | collective-permute-start | bytes 7077896 | tf_op jit(solution)/shard_map/ppermute | solution.py:275
  161.5 115.5 %copy-start.5 = (bf16[512,768]{1,0:T(8,128)(2,1)}, bf16[512,768]{1,0:T(8,128)(2,1)S(1)}, u32[]{:S(2)}) copy-start(bf16[512,768]{1,0:T(8,128)(2,1)S(1)} %get-tuple-element.110.refs_0_) | copy-start | bytes 2359300
  161.5 15.7 %copy-start.14 = (bf16[768,192]{1,0:T(8,128)(2,1)S(1)}, bf16[768,192]{1,0:T(8,128)(2,1)}, u32[]{:S(2)}) copy-start(bf16[768,192]{1,0:T(8,128)(2,1)} %copy-done.13) | copy-start | bytes 884740
  161.5 15.7 %copy-start.16 = (bf16[768,192]{1,0:T(8,128)(2,1)S(1)}, bf16[768,192]{1,0:T(8,128)(2,1)}, u32[]{:S(2)}) copy-start(bf16[768,192]{1,0:T(8,128)(2,1)} %copy-done.15) | copy-start | bytes 884740
  177.0 29.8 %collective-permute-start.31 = (bf16[768,768]{1,0:T(8,128)(2,1)}, bf16[768,768]{1,0:T(8,128)(2,1)}, u32[]{:S(2)}, u32[]{:S(2)}) collective-permute-start(bf16[768,768]{1,0:T(8,128)(2,1)} %get-tuple-element.131), channel_id=1, source_target_pairs={{0,1},{1,0},{2,3},{3,2},{4,5},{5,4},{6,7},{7,6},{8,9},{9,8},{10,11... | collective-permute-start | bytes 3538952 | tf_op jit(solution)/shard_map/ppermute | solution.py:275
  194.5 12.2 %copy-start.33 = (bf16[768,768]{1,0:T(8,128)(2,1)S(1)}, bf16[768,768]{1,0:T(8,128)(2,1)}, u32[]{:S(2)}) copy-start(bf16[768,768]{1,0:T(8,128)(2,1)} %get-tuple-element.130) | copy-start | bytes 3538948
  195.7 29.2 %copy-start.6 = (bf16[512,768]{1,0:T(8,128)(2,1)}, bf16[512,768]{1,0:T(8,128)(2,1)S(1)}, u32[]{:S(2)}) copy-start(bf16[512,768]{1,0:T(8,128)(2,1)S(1)} %get-tuple-element.127.refs_0_) | copy-start | bytes 2359300
  195.8 1.3 collective-permute-start.36
  196.2 13.7 %collective-permute-start.27 = (bf16[768,768]{1,0:T(8,128)(2,1)}, bf16[768,768]{1,0:T(8,128)(2,1)}, u32[]{:S(2)}, u32[]{:S(2)}) collective-permute-start(bf16[768,768]{1,0:T(8,128)(2,1)} %get-tuple-element.129), channel_id=1, source_target_pairs={{0,1},{1,0},{2,3},{3,2},{4,5},{5,4},{6,7},{7,6},{8,9},{9,8},{10,11... | collective-permute-start | bytes 3538952 | tf_op jit(solution)/shard_map/ppermute | solution.py:275
  197.2 3.9 collective-permute-start.37
  201.1 3.9 collective-permute-start.38
  202.9 59.6 %collective-permute-start.41 = (bf16[768,1536]{1,0:T(8,128)(2,1)}, bf16[768,1536]{1,0:T(8,128)(2,1)}, u32[]{:S(2)}, u32[]{:S(2)}) collective-permute-start(bf16[768,1536]{1,0:T(8,128)(2,1)} %get-tuple-element.140), channel_id=1, source_target_pairs={{0,1},{1,0},{2,3},{3,2},{4,5},{5,4},{6,7},{7,6},{8,9},{9,8},{10,11... | collective-permute-start | bytes 7077896 | tf_op jit(solution)/shard_map/ppermute | solution.py:275
  205.0 14.2 %collective-permute-start.39 = (f32[8,768]{1,0:T(8,128)S(1)}, f32[8,768]{1,0:T(8,128)S(1)}, u32[]{:S(2)}, u32[]{:S(2)}) collective-permute-start(f32[8,768]{1,0:T(8,128)S(1)} %add.164), channel_id=1, source_target_pairs={{0,8},{4,12},{8,0},{12,4},{16,24},{20,28},{24,16},{28,20},{1,9},{5... | collective-permute-start | bytes 73736 | tf_op jit(solution)/shard_map/ppermute | solution.py:275
  208.4 16.4 %collective-permute-start.32 = (bf16[4,96,768]{2,1,0:T(8,128)(2,1)S(1)}, bf16[4,96,768]{2,1,0:T(8,128)(2,1)}, u32[]{:S(2)}, u32[]{:S(2)}) collective-permute-start(bf16[4,96,768]{2,1,0:T(8,128)(2,1)S(1)} %dynamic-slice_bitcast_fusion.4), channel_id=1, source_target_pairs={{0,4},{4,0},{8,12},{12,8},{16,20},{20,16},{24,28},{28,24},{1,5},{5... | collective-permute-start | bytes 1769480 | tf_op jit(solution)/shard_map/ppermute | solution.py:275
  212.8 21.6 %collective-permute-start.28 = (bf16[4,96,768]{2,1,0:T(8,128)(2,1)}, bf16[4,96,768]{2,1,0:T(8,128)(2,1)}, u32[]{:S(2)}, u32[]{:S(2)}) collective-permute-start(bf16[4,96,768]{2,1,0:T(8,128)(2,1)} %dynamic-slice_bitcast_fusion.5), channel_id=1, source_target_pairs={{0,4},{4,0},{8,12},{12,8},{16,20},{20,16},{24,28},{28,24},{1,5},{5... | collective-permute-start | bytes 1769480 | tf_op jit(solution)/shard_map/ppermute | solution.py:275
  217.6 45.4 %collective-permute-start.43 = (bf16[768,768]{1,0:T(8,128)(2,1)}, bf16[768,768]{1,0:T(8,128)(2,1)}, u32[]{:S(2)}, u32[]{:S(2)}) collective-permute-start(bf16[768,768]{1,0:T(8,128)(2,1)} %get-tuple-element.185), channel_id=1, source_target_pairs={{0,2},{1,3},{2,0},{3,1},{4,6},{5,7},{6,4},{7,5},{8,10},{9,11},{10,... | collective-permute-start | bytes 3538952 | tf_op jit(solution)/shard_map/ppermute | solution.py:275
  219.1 4.9 collective-permute-start.40
  224.1 36.7 %collective-permute-start.25 = (bf16[512,768]{1,0:T(8,128)(2,1)S(1)}, bf16[512,768]{1,0:T(8,128)(2,1)}, u32[]{:S(2)}, u32[]{:S(2)}) collective-permute-start(bf16[512,768]{1,0:T(8,128)(2,1)S(1)} %get-tuple-element.127.refs_0_), channel_id=1, source_target_pairs={{0,2},{1,3},{2,0},{3,1},{4,6},{5,7},{6,4},{7,5},{8,10},{9,11},{10,... | collective-permute-start | bytes 2359304 | tf_op jit(solution)/shard_map/ppermute | solution.py:275
  224.6 10.3 %copy-start.28 = (bf16[768,768]{1,0:T(8,128)(2,1)S(1)}, bf16[768,768]{1,0:T(8,128)(2,1)}, u32[]{:S(2)}) copy-start(bf16[768,768]{1,0:T(8,128)(2,1)} %copy-done.27) | copy-start | bytes 3538948
  224.9 53.6 %collective-permute-start.24 = (bf16[512,768]{1,0:T(8,128)(2,1)S(1)}, bf16[512,768]{1,0:T(8,128)(2,1)S(1)}, u32[]{:S(2)}, u32[]{:S(2)}) collective-permute-start(bf16[512,768]{1,0:T(8,128)(2,1)S(1)} %get-tuple-element.127.refs_0_), channel_id=1, source_target_pairs={{0,1},{1,0},{2,3},{3,2},{4,5},{5,4},{6,7},{7,6},{8,9},{9,8},{10,11... | collective-permute-start | bytes 2359304 | tf_op jit(solution)/shard_map/ppermute | solution.py:275
  234.4 27.9 %collective-permute-start.33 = (bf16[2,96,768]{2,1,0:T(8,128)(2,1)S(1)}, bf16[2,96,768]{2,1,0:T(8,128)(2,1)S(1)}, u32[]{:S(2)}, u32[]{:S(2)}) collective-permute-start(bf16[2,96,768]{2,1,0:T(8,128)(2,1)S(1)} %dynamic-slice_bitcast_fusion.7), channel_id=1, source_target_pairs={{0,8},{4,12},{8,0},{12,4},{16,24},{20,28},{24,16},{28,20},{1,9},{5... | collective-permute-start | bytes 884744 | tf_op jit(solution)/shard_map/ppermute | solution.py:275
  234.9 30.7 %copy-start.32 = (bf16[768,1536]{1,0:T(8,128)(2,1)S(1)}, bf16[768,1536]{1,0:T(8,128)(2,1)}, u32[]{:S(2)}) copy-start(bf16[768,1536]{1,0:T(8,128)(2,1)} %get-tuple-element.139) | copy-start | bytes 7077892
  260.8 16.2 %collective-permute-start.22 = (bf16[512,768]{1,0:T(8,128)(2,1)S(1)}, bf16[512,768]{1,0:T(8,128)(2,1)}, u32[]{:S(2)}, u32[]{:S(2)}) collective-permute-start(bf16[512,768]{1,0:T(8,128)(2,1)S(1)} %get-tuple-element.110.refs_0_), channel_id=1, source_target_pairs={{0,2},{1,3},{2,0},{3,1},{4,6},{5,7},{6,4},{7,5},{8,10},{9,11},{10,... | collective-permute-start | bytes 2359304 | tf_op jit(solution)/shard_map/ppermute | solution.py:275
  262.3 19.6 %collective-permute-start.26 = (bf16[512,768]{1,0:T(8,128)(2,1)}, bf16[512,768]{1,0:T(8,128)(2,1)}, u32[]{:S(2)}, u32[]{:S(2)}) collective-permute-start(bf16[512,768]{1,0:T(8,128)(2,1)} %collective-permute-done.25.refs_2_), channel_id=1, source_target_pairs={{0,1},{1,0},{2,3},{3,2},{4,5},{5,4},{6,7},{7,6},{8,9},{9,8},{10,11... | collective-permute-start | bytes 2359304 | tf_op jit(solution)/shard_map/ppermute | solution.py:275
  262.5 14.6 %collective-permute-start.29 = (bf16[2,96,768]{2,1,0:T(8,128)(2,1)S(1)}, bf16[2,96,768]{2,1,0:T(8,128)(2,1)S(1)}, u32[]{:S(2)}, u32[]{:S(2)}) collective-permute-start(bf16[2,96,768]{2,1,0:T(8,128)(2,1)S(1)} %dynamic-slice_bitcast_fusion.8), channel_id=1, source_target_pairs={{0,8},{4,12},{8,0},{12,4},{16,24},{20,28},{24,16},{28,20},{1,9},{5... | collective-permute-start | bytes 884744 | tf_op jit(solution)/shard_map/ppermute | solution.py:275
  263.0 14.5 %collective-permute-start.34 = (bf16[1,96,768]{2,1,0:T(8,128)(2,1)S(1)}, bf16[1,96,768]{2,1,0:T(8,128)(2,1)S(1)}, u32[]{:S(2)}, u32[]{:S(2)}) collective-permute-start(bf16[1,96,768]{2,1,0:T(8,128)(2,1)S(1)} %constant_dynamic-slice_fusion.2), channel_id=1, source_target_pairs={{0,16},{4,20},{8,24},{12,28},{16,0},{20,4},{24,8},{28,12},{1,17},{... | collective-permute-start | bytes 442376 | tf_op jit(solution)/shard_map/ppermute | solution.py:275
  277.0 104.1 %collective-permute-start.21 = (bf16[512,768]{1,0:T(8,128)(2,1)S(1)}, bf16[512,768]{1,0:T(8,128)(2,1)}, u32[]{:S(2)}, u32[]{:S(2)}) collective-permute-start(bf16[512,768]{1,0:T(8,128)(2,1)S(1)} %get-tuple-element.110.refs_0_), channel_id=1, source_target_pairs={{0,1},{1,0},{2,3},{3,2},{4,5},{5,4},{6,7},{7,6},{8,9},{9,8},{10,11... | collective-permute-start | bytes 2359304 | tf_op jit(solution)/shard_map/ppermute | solution.py:275
  277.0 104.2 %collective-permute-start.23 = (bf16[512,768]{1,0:T(8,128)(2,1)}, bf16[512,768]{1,0:T(8,128)(2,1)}, u32[]{:S(2)}, u32[]{:S(2)}) collective-permute-start(bf16[512,768]{1,0:T(8,128)(2,1)} %collective-permute-done.22.refs_2_), channel_id=1, source_target_pairs={{0,1},{1,0},{2,3},{3,2},{4,5},{5,4},{6,7},{7,6},{8,9},{9,8},{10,11... | collective-permute-start | bytes 2359304 | tf_op jit(solution)/shard_map/ppermute | solution.py:275
  277.5 201.6 %collective-permute-start.47 = (bf16[2,4,96,768]{3,2,1,0:T(8,128)(2,1)}, bf16[2,4,96,768]{3,2,1,0:T(8,128)(2,1)}, u32[]{:S(2)}, u32[]{:S(2)}) collective-permute-start(bf16[2,4,96,768]{3,2,1,0:T(8,128)(2,1)} %fusion.2), channel_id=1, source_target_pairs={{0,4},{4,0},{8,12},{12,8},{16,20},{20,16},{24,28},{28,24},{1,5},{5... | collective-permute-start | bytes 3538952 | tf_op jit(solution)/shard_map/ppermute | solution.py:275
  279.3 198.3 %collective-permute-start.30 = (bf16[1,96,768]{2,1,0:T(8,128)(2,1)S(1)}, bf16[1,96,768]{2,1,0:T(8,128)(2,1)S(1)}, u32[]{:S(2)}, u32[]{:S(2)}) collective-permute-start(bf16[1,96,768]{2,1,0:T(8,128)(2,1)S(1)} %constant_dynamic-slice_fusion.3), channel_id=1, source_target_pairs={{0,16},{4,20},{8,24},{12,28},{16,0},{20,4},{24,8},{28,12},{1,17},{... | collective-permute-start | bytes 442376 | tf_op jit(solution)/shard_map/ppermute | solution.py:275
  281.9 195.7 %collective-permute-start.35 = (bf16[96,768]{1,0:T(8,128)(2,1)S(1)}, bf16[96,768]{1,0:T(8,128)(2,1)S(1)}, u32[]{:S(2)}, u32[]{:S(2)}) collective-permute-start(bf16[96,768]{1,0:T(8,128)(2,1)S(1)} %fusion.14), channel_id=1, source_target_pairs={{0,2},{1,3},{2,0},{3,1},{4,6},{5,7},{6,4},{7,5},{8,10},{9,11},{10,... | collective-permute-start | bytes 442376 | tf_op jit(solution)/shard_map/ppermute | solution.py:275
  381.2 96.6 %copy-start.29 = (bf16[768,768]{1,0:T(8,128)(2,1)S(1)}, bf16[768,768]{1,0:T(8,128)(2,1)}, u32[]{:S(2)}) copy-start(bf16[768,768]{1,0:T(8,128)(2,1)} %get-tuple-element.187) | copy-start | bytes 3538948
  477.8 14.6 %collective-permute-start.44 = (bf16[4,96,768]{2,1,0:T(8,128)(2,1)S(1)}, bf16[4,96,768]{2,1,0:T(8,128)(2,1)}, u32[]{:S(2)}, u32[]{:S(2)}) collective-permute-start(bf16[4,96,768]{2,1,0:T(8,128)(2,1)S(1)} %dynamic-slice_bitcast_fusion.3), channel_id=1, source_target_pairs={{0,4},{4,0},{8,12},{12,8},{16,20},{20,16},{24,28},{28,24},{1,5},{5... | collective-permute-start | bytes 1769480 | tf_op jit(solution)/shard_map/ppermute | solution.py:275
  480.7 11.7 %copy-start.30 = (bf16[768,768]{1,0:T(8,128)(2,1)S(1)}, bf16[768,768]{1,0:T(8,128)(2,1)}, u32[]{:S(2)}) copy-start(bf16[768,768]{1,0:T(8,128)(2,1)} %get-tuple-element.187) | copy-start | bytes 3538948
  481.6 15.9 %collective-permute-start.48 = (bf16[2,2,96,768]{3,2,1,0:T(8,128)(2,1)}, bf16[2,2,96,768]{3,2,1,0:T(8,128)(2,1)}, u32[]{:S(2)}, u32[]{:S(2)}) collective-permute-start(bf16[2,2,96,768]{3,2,1,0:T(8,128)(2,1)} %dynamic-slice_bitcast_fusion.2), channel_id=1, source_target_pairs={{0,8},{4,12},{8,0},{12,4},{16,24},{20,28},{24,16},{28,20},{1,9},{5... | collective-permute-start | bytes 1769480 | tf_op jit(solution)/shard_map/ppermute | solution.py:275
  493.7 11.9 %collective-permute-start.45 = (bf16[2,96,768]{2,1,0:T(8,128)(2,1)S(1)}, bf16[2,96,768]{2,1,0:T(8,128)(2,1)S(1)}, u32[]{:S(2)}, u32[]{:S(2)}) collective-permute-start(bf16[2,96,768]{2,1,0:T(8,128)(2,1)S(1)} %dynamic-slice_bitcast_fusion.6), channel_id=1, source_target_pairs={{0,8},{4,12},{8,0},{12,4},{16,24},{20,28},{24,16},{28,20},{1,9},{5... | collective-permute-start | bytes 884744 | tf_op jit(solution)/shard_map/ppermute | solution.py:275
  498.7 17.7 %collective-permute-start.49 = (bf16[2,1,96,768]{3,2,1,0:T(8,128)(2,1)S(1)}, bf16[2,1,96,768]{3,2,1,0:T(8,128)(2,1)S(1)}, u32[]{:S(2)}, u32[]{:S(2)}) collective-permute-start(bf16[2,1,96,768]{3,2,1,0:T(8,128)(2,1)S(1)} %constant_dynamic-slice_fusion), channel_id=1, source_target_pairs={{0,16},{4,20},{8,24},{12,28},{16,0},{20,4},{24,8},{28,12},{1,17},{... | collective-permute-start | bytes 884744 | tf_op jit(solution)/shard_map/ppermute | solution.py:275
  505.6 12.3 %collective-permute-start.46 = (bf16[1,96,768]{2,1,0:T(8,128)(2,1)S(1)}, bf16[1,96,768]{2,1,0:T(8,128)(2,1)S(1)}, u32[]{:S(2)}, u32[]{:S(2)}) collective-permute-start(bf16[1,96,768]{2,1,0:T(8,128)(2,1)S(1)} %constant_dynamic-slice_fusion.1), channel_id=1, source_target_pairs={{0,16},{4,20},{8,24},{12,28},{16,0},{20,4},{24,8},{28,12},{1,17},{... | collective-permute-start | bytes 442376 | tf_op jit(solution)/shard_map/ppermute | solution.py:275
  516.5 5.2 collective-permute-start.50
  (31 other events, 105.2 us)
